TPU v7x, 32 devices: a whole 2x2x4 slice. The times are simulated.
32 devices in a mesh: days: 4 (over y, x), assets: 8 (over z, core).
Axes of the slice: x: 2, y: 2, z: 4, core: 2. Of those that a mesh axis runs over, the one named last changes fastest.
Arguments:
- factors: bfloat16 [768, 256], P('days'), may hold values from -6 to 6
- returns: bfloat16 [768, 16384], P('days', 'assets'), may hold values from -6 to 6
Outputs:
- loadings: float32 [256, 16384], P(None, 'assets')
- covariance: float32 [16384, 16384], P('assets', 'days')
All inputs are finite; a program needn't handle non-finite values.
Results may differ from a plain program's by a relative error of at most 0.0036.
Values may be sent and summed in bfloat16 or wider, within the bound.
No kernel may reach another device: no remote copies, remote signals or barrier semaphores. Data moves between devices by JAX's collectives and lax.ppermute only.
A program may use at most 128 MiB of HBM per device.

v0:
```python
import functools

import jax
import jax.numpy as jnp
from jax import lax
from jax.experimental import pallas as pl
from jax.experimental.pallas import tpu as pltpu
from jax.sharding import PartitionSpec as P


AXES = ("days", "assets")
NB = 64
STEPS = 24
CHUNKS = (1, 1)
BF, F32 = jnp.bfloat16, jnp.float32
VMEM_ALL = 67043328
HIGHEST = lax.Precision.HIGHEST


def dot(a, b, dims=((1,), (0,)), precision=None):
    return lax.dot_general(a, b, (dims, ((), ())), precision=precision, preferred_element_type=F32)


def cost(flops, nbytes):
    return pl.CostEstimate(flops=int(flops), bytes_accessed=int(nbytes), transcendentals=0)


def small_inverse(block):
    n = block.shape[0]
    row = lax.broadcasted_iota(jnp.int32, (n, n), 0)
    col = lax.broadcasted_iota(jnp.int32, (n, n), 1)
    for k in range(n):
        pivot = 1.0 / block[k : k + 1, k : k + 1]
        r = jnp.where(col[:1] == k, 1.0, block[k : k + 1, :]) * pivot
        c = jnp.where(row[:, :1] == k, -1.0, block[:, k : k + 1])
        block = jnp.where((row == k) | (col == k), 0.0, block) - c * r
    return block


def sweep(a, b):
    size = a.shape[0]
    lo, hi = b * NB, (b + 1) * NB
    wide = lambda shape, axis: lax.broadcasted_iota(jnp.int32, shape, axis)
    inverse = small_inverse(a[lo:hi, lo:hi])
    across = wide((NB, size), 1) - lo
    unit = jnp.where(wide((NB, size), 0) == across, 1.0, 0.0)
    across = dot(inverse, jnp.where((across >= 0) & (across < NB), unit, a[lo:hi, :]), precision=HIGHEST)
    rows = wide((size, NB), 0) - lo
    unit = jnp.where(rows == wide((size, NB), 1), -1.0, 0.0)
    down = jnp.where((rows >= 0) & (rows < NB), unit, a[:, lo:hi])
    row, col = wide((size, size), 0), wide((size, size), 1)
    inside = ((row >= lo) & (row < hi)) | ((col >= lo) & (col < hi))
    a[...] = jnp.where(inside, 0.0, a[...]) - dot(down, across, precision=HIGHEST)


def split(a):
    high = a.astype(BF)
    return high, (a - high.astype(F32)).astype(BF)


def dot3(a, b):
    return dot(a[0], b[0]) + dot(a[0], b[1]) + dot(a[1], b[0])


def invert_kernel(n, order, *refs):
    pieces = refs[:n]
    full, high, low, gram, x = refs[n:]
    depth, size = pieces[0].shape
    for j in range(n):
        full[pl.ds(pl.multiple_of(order[j] * depth, depth), depth), :] = pieces[j][...]
    gram[...] = dot(full[...], full[...], ((0,), (0,)))

    parts = split(gram[...])
    row = lax.broadcasted_iota(jnp.int32, (size, size), 0)
    col = lax.broadcasted_iota(jnp.int32, (size, size), 1)
    eye = jnp.where(row == col, 1.0, 0.0)
    bound = jnp.max(jnp.sum(jnp.abs(gram[...]), axis=0, keepdims=True), axis=1, keepdims=True)
    x[...] = eye * (1.0 / bound)

    def step():
        at = split(x[...])
        rest = eye - dot3(parts, at)
        x[...] = x[...] + dot3(at, split(rest))
        return rest

    for _ in range(4):
        step()

    def body(carry):
        rest = step()
        return carry[0] + 1, jnp.sum(rest * rest)

    def going(carry):
        return (carry[0] < STEPS) & jnp.logical_not(carry[1] < 1e-4)

    _, error = lax.while_loop(going, body, (0, jnp.float32(1.0)))
    done = error < 1e-4

    @pl.when(done)
    def _():
        rest = eye - dot(gram[...], x[...], precision=HIGHEST)
        x[...] = x[...] + dot(x[...], rest, precision=HIGHEST)

    @pl.when(jnp.logical_not(done))
    def _():
        x[...] = gram[...]
        for b in range(size // NB):
            sweep(x, b)

    h = dot(x[...], full[...].astype(F32), ((1,), (1,)), precision=HIGHEST)
    high[...], low[...] = split(h)


def invert(order, pieces):
    n = len(pieces)
    depth, size = pieces[0].shape
    days = n * depth
    return pl.pallas_call(
        functools.partial(invert_kernel, n),
        in_specs=[pl.BlockSpec(memory_space=pltpu.SMEM)] + [pl.BlockSpec(memory_space=pltpu.VMEM)] * n,
        out_shape=[jax.ShapeDtypeStruct((days, size), BF)] + [jax.ShapeDtypeStruct((size, days), BF)] * 2,
        scratch_shapes=[pltpu.VMEM((size, size), F32)] * 2,
        cost_estimate=cost(2e10, 8 * days * size),
        compiler_params=pltpu.CompilerParams(vmem_limit_bytes=VMEM_ALL),
        name="gram",
    )(order, *pieces)


def residual_kernel(n, halves, with_loadings, order, *refs):
    tiles = pl.num_programs(0)
    count = n + 1 if halves else n
    pieces = refs[:count]
    high, low, factors = refs[count : count + 3]
    outs = refs[count + 3 : -1]
    y = refs[-1]
    depth = pieces[0].shape[0]

    def put(j, ref):
        y[pl.ds(pl.multiple_of(order[j] * depth, depth), depth), :] = ref[...]

    for j in range(n - 1 if halves else n):
        put(j, pieces[j])
    if halves:
        left = pl.program_id(0) < tiles // 2

        @pl.when(left)
        def _():
            put(n - 1, pieces[n - 1])

        @pl.when(jnp.logical_not(left))
        def _():
            put(n - 1, pieces[n])

    loadings = dot(high[...], y[...]) + dot(low[...], y[...])
    fitted = dot(factors[...], loadings.astype(BF))
    outs[0][...] = (y[...].astype(F32) - fitted).astype(BF)
    if with_loadings:
        outs[1][...] = loadings


def residuals(order, pieces, high, low, factors, width, with_loadings, halves=False, tile=512):
    n = len(pieces) - 1 if halves else len(pieces)
    depth = pieces[0].shape[0]
    size, days = high.shape
    tile = min(tile, width // 2 if halves else width)
    tiles = width // tile
    spec = pl.BlockSpec((depth, tile), lambda i, order: (0, i))
    specs = [spec] * n
    if halves:
        half = tiles // 2
        specs = specs[:-1] + [
            pl.BlockSpec((depth, tile), lambda i, order: (0, jnp.minimum(i, half - 1))),
            pl.BlockSpec((depth, tile), lambda i, order: (0, jnp.maximum(i - half, 0))),
        ]
    whole = lambda shape: pl.BlockSpec(shape, lambda i, order: (0, 0))
    out_specs = [pl.BlockSpec((days, tile), lambda i, order: (0, i))]
    out_shape = [jax.ShapeDtypeStruct((days, width), BF)]
    if with_loadings:
        out_specs.append(pl.BlockSpec((size, tile), lambda i, order: (0, i)))
        out_shape.append(jax.ShapeDtypeStruct((size, width), F32))
    return pl.pallas_call(
        functools.partial(residual_kernel, n, halves, with_loadings),
        grid_spec=pltpu.PrefetchScalarGridSpec(
            num_scalar_prefetch=1,
            grid=(tiles,),
            in_specs=specs + [whole((size, days))] * 2 + [whole((days, size))],
            out_specs=out_specs,
            scratch_shapes=[pltpu.VMEM((days, tile), BF)],
        ),
        out_shape=out_shape,
        cost_estimate=cost(6 * days * size * width, 4 * days * width),
        compiler_params=pltpu.CompilerParams(vmem_limit_bytes=VMEM_ALL),
        name="residual",
    )(order, *pieces, high, low, factors)


def covariance_kernel(scale, count, where, rows, *refs):
    out = refs[-1]
    step = pl.program_id(0)
    for k in range(count):
        @pl.when(step == k if count > 1 else step >= 0)
        def _():
            out[...] = dot(rows[...], refs[k][...], ((0,), (0,))) * scale


def covariance(held, rows, parts, starts, total, days, tile=512):
    depth, height = rows.shape
    width = parts[0].shape[1]
    tile = min(tile, width)
    count, tiles = len(parts), width // tile
    specs = [pl.BlockSpec((depth, height), lambda k, j, where: (0, 0))]
    for k in range(count):
        held_at = lambda s, j, where, k=k: (0, jnp.where(s == k, j, jnp.where(s < k, 0, tiles - 1)))
        specs.append(pl.BlockSpec((depth, tile), held_at))
    args = [rows, *parts]
    aliases = {}
    if held is not None:
        specs.append(pl.BlockSpec(memory_space=pl.ANY))
        args.append(held)
        aliases = {len(args): 0}
    return pl.pallas_call(
        functools.partial(covariance_kernel, 1.0 / days, count),
        grid_spec=pltpu.PrefetchScalarGridSpec(
            num_scalar_prefetch=1,
            grid=(count, tiles),
            in_specs=specs,
            out_specs=pl.BlockSpec((height, tile), lambda k, j, where: (0, where[k] + j)),
        ),
        out_shape=jax.ShapeDtypeStruct((height, total), F32),
        input_output_aliases=aliases,
        cost_estimate=cost(2 * depth * height * width * count, 4 * height * width * count),
        compiler_params=pltpu.CompilerParams(vmem_limit_bytes=VMEM_ALL),
        name="covariance",
    )(jnp.stack([lax.div(s, tile) for s in starts]).astype(jnp.int32), *args)


def per_device(nd, na, factors, returns):
    reps = na // nd
    depth, width = returns.shape
    days = depth * nd
    xor = nd & (nd - 1) == 0

    def mix(i, k, j):
        return i ^ k ^ j if xor else (i + k + j) % nd

    def move(x, target):
        pairs = []
        for d in range(nd):
            for a in range(na):
                to = target(d, a // reps, a % reps)
                pairs.append((d * na + a, to[0] * na + to[1] * reps + to[2]))
        return lax.ppermute(x, AXES, pairs)

    def shift(i, j):
        return i ^ j if xor else (i + j) % nd

    def unshift(i, j):
        return i ^ j if xor else (i - j + nd) % nd

    d = lax.axis_index("days")
    a = lax.axis_index("assets")
    q, c = lax.div(a, reps), lax.rem(a, reps)
    order = jnp.stack([unshift(d, j) for j in range(nd)]).astype(jnp.int32)
    col_order = jnp.stack([mix(q, d, j) if xor else (q - d - j + 2 * nd) % nd for j in range(nd)]).astype(jnp.int32)

    def plane(x, j):
        return move(x, lambda d, q, c: (shift(d, j), q, c))

    factor_pieces = [factors] + [plane(factors, j) for j in range(1, nd)]
    row_pieces = [returns] + [plane(returns, j) for j in range(1, nd)]

    sizes = [width * s // sum(CHUNKS) for s in CHUNKS]
    starts = [sum(sizes[:i]) for i in range(len(sizes))]
    top = nd // 2 if xor and nd > 1 else 0
    chunk_pieces = []
    for start, size in zip(starts, sizes):
        x = lax.optimization_barrier(returns[:, start : start + size])
        if top:
            far = move(x, lambda d, q, c: (d, q ^ top, c))
            flip = (d & top) != 0
            sends = [jnp.where(flip, far, x), jnp.where(flip, x, far)]
        pieces = []
        for j in range(nd):
            if top:
                target = lambda d, q, c, j=j: (q ^ ((d ^ j) & top), q ^ ((d ^ j) & ~top), c)
                pieces.append(move(sends[1 if j & top else 0], target))
            else:
                pieces.append(move(x, lambda d, q, c, j=j: (q, mix(q, d, j), c)))
        chunk_pieces.append(pieces)

    full, high, low = invert(order, factor_pieces)
    rows, loadings = residuals(order, row_pieces, high, low, full, width, True)

    held = None
    total = reps * width
    for i, (start, pieces) in enumerate(zip(starts, chunk_pieces)):
        (cols,) = residuals(col_order, pieces, high, low, full, sizes[i], False)
        parts, at = [], []
        for s in range(reps):
            parts.append(cols if s == 0 else move(cols, lambda d, q, c: (d, q, (c - s) % reps)))
            at.append(lax.rem(c + s, reps) * width + start)
        last = i == len(sizes) - 1
        groups = [[s] for s in range(reps)] if last else [list(range(reps))]
        for group in groups:
            held = covariance(held, rows, [parts[s] for s in group], [at[s] for s in group], total, days)
    return loadings, held


def solution(mesh):
    nd, na = mesh.shape["days"], mesh.shape["assets"]

    def body(factors, returns):
        return per_device(nd, na, factors, returns)

    return jax.shard_map(
        body,
        mesh=mesh,
        in_specs=(P("days", None), P("days", "assets")),
        out_specs=(P(None, "assets"), P("assets", "days")),
        check_vma=False,
    )
```

profile of v0, /device:TPU:16, one launch (start us, length us, event | category | flops | bytes accessed | tf_op | source)
XLA Modules:
  0.0 169.1 jit_solution(16151486984596535803)
XLA Ops:
  0.6 1.9 %fusion = (bf16[192,1024]{1,0:T(8,128)(2,1)S(1)}, bf16[192,1024]{1,0:T(8,128)(2,1)}) fusion(bf16[192,2048]{1,0:T(8,128)(2,1)} %refs_0_.3), kind=kLoop, calls=%fused_computation.7 | loop fusion | bytes 1572864 | tf_op jit(solution)/shard_map/slice | solution.py:277
  2.5 0.0 collective-permute-start.12
  2.5 1.8 %collective-permute-start.3 = (bf16[192,256]{1,0:T(8,128)(2,1)}, bf16[192,256]{1,0:T(8,128)(2,1)}, u32[]{:S(2)}, u32[]{:S(2)}) collective-permute-start(bf16[192,256]{1,0:T(8,128)(2,1)} %refs_0_.2), channel_id=1, source_target_pairs={{0,8},{1,9},{2,10},{3,11},{4,12},{5,13},{6,14},{7,15},{8,0},{9,1},... | collective-permute-start | bytes 294920 | tf_op jit(solution)/shard_map/ppermute | solution.py:252
  4.4 1.5 collective-permute-start.4
  5.9 0.1 collective-permute-start.5
  6.0 2.9 %collective-permute-start.6 = (bf16[192,1024]{1,0:T(8,128)(2,1)}, bf16[192,1024]{1,0:T(8,128)(2,1)}, u32[]{:S(2)}, u32[]{:S(2)}) collective-permute-start(bf16[192,1024]{1,0:T(8,128)(2,1)} %get-tuple-element.15), channel_id=1, source_target_pairs={{0,4},{1,5},{2,6},{3,7},{4,0},{5,1},{6,2},{7,3},{8,12},{9,13},{10,... | collective-permute-start | bytes 1179656 | tf_op jit(solution)/shard_map/ppermute | solution.py:252
  9.0 0.6 pad_add_fusion.1.order
  9.5 0.6 pad_add_fusion.order
  10.1 18.8 %collective-permute-done.12 = bf16[192,1024]{1,0:T(8,128)(2,1)S(1)} collective-permute-done((bf16[192,1024]{1,0:T(8,128)(2,1)S(1)}, bf16[192,1024]{1,0:T(8,128)(2,1)S(1)}, u32[]{:S(2)}, u32[]{:S(2)}) %collective-permute-start.12) | collective-permute-done | bytes 393248 | tf_op jit(solution)/shard_map/ppermute | solution.py:252
  28.9 0.9 broadcast_select_fusion
  29.8 3.7 %collective-permute-start.13 = (bf16[192,1024]{1,0:T(8,128)(2,1)}, bf16[192,1024]{1,0:T(8,128)(2,1)}, u32[]{:S(2)}, u32[]{:S(2)}) collective-permute-start(bf16[192,1024]{1,0:T(8,128)(2,1)} %get-tuple-element.13), channel_id=1, source_target_pairs={{0,0},{1,1},{2,10},{3,11},{4,20},{5,21},{6,30},{7,31},{8,2},{9,3},... | collective-permute-start | bytes 1179656 | tf_op jit(solution)/shard_map/ppermute | solution.py:252
  33.6 0.0 collective-permute-done.3.refs_1_
  33.6 6.3 %collective-permute-start.14 = (bf16[192,1024]{1,0:T(8,128)(2,1)}, bf16[192,1024]{1,0:T(8,128)(2,1)}, u32[]{:S(2)}, u32[]{:S(2)}) collective-permute-start(bf16[192,1024]{1,0:T(8,128)(2,1)} %get-tuple-element.13), channel_id=1, source_target_pairs={{0,2},{1,3},{2,8},{3,9},{4,22},{5,23},{6,28},{7,29},{8,0},{9,1},{1... | collective-permute-start | bytes 1179656 | tf_op jit(solution)/shard_map/ppermute | solution.py:252
  39.9 0.0 collective-permute-done.4.refs_2_
  39.9 4.5 %collective-permute-start.15 = (bf16[192,1024]{1,0:T(8,128)(2,1)}, bf16[192,1024]{1,0:T(8,128)(2,1)}, u32[]{:S(2)}, u32[]{:S(2)}) collective-permute-start(bf16[192,1024]{1,0:T(8,128)(2,1)} %get-tuple-element.12), channel_id=1, source_target_pairs={{0,16},{1,17},{2,26},{3,27},{4,4},{5,5},{6,14},{7,15},{8,18},{9,19... | collective-permute-start | bytes 1179656 | tf_op jit(solution)/shard_map/ppermute | solution.py:252
  44.4 0.0 collective-permute-done.5.refs_3_
  44.4 1.9 %collective-permute-start.16 = (bf16[192,1024]{1,0:T(8,128)(2,1)}, bf16[192,1024]{1,0:T(8,128)(2,1)}, u32[]{:S(2)}, u32[]{:S(2)}) collective-permute-start(bf16[192,1024]{1,0:T(8,128)(2,1)} %get-tuple-element.12), channel_id=1, source_target_pairs={{0,18},{1,19},{2,24},{3,25},{4,6},{5,7},{6,12},{7,13},{8,16},{9,17... | collective-permute-start | bytes 1179656 | tf_op jit(solution)/shard_map/ppermute | solution.py:252
  46.3 12.6 %gram.1 = (bf16[768,256]{1,0:T(8,128)(2,1)}, bf16[256,768]{1,0:T(8,128)(2,1)}, bf16[256,768]{1,0:T(8,128)(2,1)}) custom-call(s32[4]{0:T(128)} %pad_add_fusion.order, bf16[192,256]{1,0:T(8,128)(2,1)} %refs_0_.2, bf16[192,256]{1,0:T(8,128)(2,1)} %collective-permute-done.3.refs_1_, bf16[192,256]{1,0:T(8,128)(2,1)} %collective-permute-done.4.refs_2_, ...), custom_call_target="tpu_custom_call" | custom-call | flops 20000000000 | bytes 1572864 | tf_op jit(solution)/shard_map/gram/pallas_call | solution.py:118
  58.9 0.0 collective-permute-done.13.refs_0_
  58.9 0.0 collective-permute-done.14.refs_1_
  58.9 0.0 collective-permute-done.15.refs_2_
  58.9 5.5 %collective-permute-done.16.refs_3_ = bf16[192,1024]{1,0:T(8,128)(2,1)} collective-permute-done((bf16[192,1024]{1,0:T(8,128)(2,1)}, bf16[192,1024]{1,0:T(8,128)(2,1)}, u32[]{:S(2)}, u32[]{:S(2)}) %collective-permute-start.16) | collective-permute-done | bytes 393248 | tf_op jit(solution)/shard_map/ppermute | solution.py:252
  64.4 5.2 %residual.5.refs_0_ = bf16[768,1024]{1,0:T(8,128)(2,1)} custom-call(s32[4]{0:T(128)} %pad_add_fusion.1.order, bf16[192,1024]{1,0:T(8,128)(2,1)} %collective-permute-done.13.refs_0_, bf16[192,1024]{1,0:T(8,128)(2,1)} %collective-permute-done.14.refs_1_, bf16[192,1024]{1,0:T(8,128)(2,1)} %collective-permute-done.15.refs_2_, ...), custom_call_target="tpu_custom_call" | custom-call | flops 1207959552 | bytes 3145728 | tf_op jit(solution)/shard_map/residual/pallas_call | solution.py:181
  69.6 0.0 collective-permute-start.17
  69.6 0.0 collective-permute-done.6
  69.7 1.2 broadcast_select_fusion.2
  70.8 4.4 %collective-permute-start.10 = (bf16[192,1024]{1,0:T(8,128)(2,1)S(1)}, bf16[192,1024]{1,0:T(8,128)(2,1)S(1)}, u32[]{:S(2)}, u32[]{:S(2)}) collective-permute-start(bf16[192,1024]{1,0:T(8,128)(2,1)S(1)} %get-tuple-element.16), channel_id=1, source_target_pairs={{0,18},{1,19},{2,24},{3,25},{4,6},{5,7},{6,12},{7,13},{8,16},{9,17... | collective-permute-start | bytes 1179656 | tf_op jit(solution)/shard_map/ppermute | solution.py:252
  75.2 3.4 %collective-permute-start.7 = (bf16[192,1024]{1,0:T(8,128)(2,1)S(1)}, bf16[192,1024]{1,0:T(8,128)(2,1)S(1)}, u32[]{:S(2)}, u32[]{:S(2)}) collective-permute-start(bf16[192,1024]{1,0:T(8,128)(2,1)S(1)} %get-tuple-element.17), channel_id=1, source_target_pairs={{0,0},{1,1},{2,10},{3,11},{4,20},{5,21},{6,30},{7,31},{8,2},{9,3},... | collective-permute-start | bytes 1179656 | tf_op jit(solution)/shard_map/ppermute | solution.py:252
  78.7 1.9 %collective-permute-start.8 = (bf16[192,1024]{1,0:T(8,128)(2,1)S(1)}, bf16[192,1024]{1,0:T(8,128)(2,1)S(1)}, u32[]{:S(2)}, u32[]{:S(2)}) collective-permute-start(bf16[192,1024]{1,0:T(8,128)(2,1)S(1)} %get-tuple-element.17), channel_id=1, source_target_pairs={{0,2},{1,3},{2,8},{3,9},{4,22},{5,23},{6,28},{7,29},{8,0},{9,1},{1... | collective-permute-start | bytes 1179656 | tf_op jit(solution)/shard_map/ppermute | solution.py:252
  80.6 1.5 collective-permute-start.9
  82.0 2.7 %collective-permute-done.10.refs_3_ = bf16[192,1024]{1,0:T(8,128)(2,1)S(1)} collective-permute-done((bf16[192,1024]{1,0:T(8,128)(2,1)S(1)}, bf16[192,1024]{1,0:T(8,128)(2,1)S(1)}, u32[]{:S(2)}, u32[]{:S(2)}) %collective-permute-start.10) | collective-permute-done | bytes 393248 | tf_op jit(solution)/shard_map/ppermute | solution.py:252
  84.7 1.9 %collective-permute-start = (bf16[192,2048]{1,0:T(8,128)(2,1)}, bf16[192,2048]{1,0:T(8,128)(2,1)}, u32[]{:S(2)}, u32[]{:S(2)}) collective-permute-start(bf16[192,2048]{1,0:T(8,128)(2,1)} %refs_0_.3), channel_id=1, source_target_pairs={{0,8},{1,9},{2,10},{3,11},{4,12},{5,13},{6,14},{7,15},{8,0},{9,1},... | collective-permute-start | bytes 2359304 | tf_op jit(solution)/shard_map/ppermute | solution.py:252
  86.6 10.1 %collective-permute-done.7.refs_0_ = bf16[192,1024]{1,0:T(8,128)(2,1)S(1)} collective-permute-done((bf16[192,1024]{1,0:T(8,128)(2,1)S(1)}, bf16[192,1024]{1,0:T(8,128)(2,1)S(1)}, u32[]{:S(2)}, u32[]{:S(2)}) %collective-permute-start.7) | collective-permute-done | bytes 393248 | tf_op jit(solution)/shard_map/ppermute | solution.py:252
  96.8 1.5 collective-permute-start.1
  98.3 0.0 collective-permute-done.8.refs_1_
  98.3 0.1 collective-permute-start.2
  98.4 0.7 copy-done.2
  99.1 0.0 collective-permute-done.9.refs_2_
  99.1 5.2 %residual.4.refs_0_ = bf16[768,1024]{1,0:T(8,128)(2,1)} custom-call(s32[4]{0:T(128)} %pad_add_fusion.1.order, bf16[192,1024]{1,0:T(8,128)(2,1)} %copy-done.1, bf16[192,1024]{1,0:T(8,128)(2,1)} %copy-done.2, bf16[192,1024]{1,0:T(8,128)(2,1)} %collective-permute-done.9.refs_2_, bf16[192,1024]{1,0:T(8,128)(2,1)} %copy-done, ...), custom_call_target="tpu_custom_call" | custom-call | flops 1207959552 | bytes 3145728 | tf_op jit(solution)/shard_map/residual/pallas_call | solution.py:181
  104.3 0.7 pad_add_fusion.2.where
  105.0 5.8 %collective-permute-done.refs_1_ = bf16[192,2048]{1,0:T(8,128)(2,1)} collective-permute-done((bf16[192,2048]{1,0:T(8,128)(2,1)}, bf16[192,2048]{1,0:T(8,128)(2,1)}, u32[]{:S(2)}, u32[]{:S(2)}) %collective-permute-start) | collective-permute-done | bytes 786464 | tf_op jit(solution)/shard_map/ppermute | solution.py:252
  110.8 22.1 %collective-permute-done.1.refs_2_ = bf16[192,2048]{1,0:T(8,128)(2,1)} collective-permute-done((bf16[192,2048]{1,0:T(8,128)(2,1)}, bf16[192,2048]{1,0:T(8,128)(2,1)}, u32[]{:S(2)}, u32[]{:S(2)}) %collective-permute-start.1) | collective-permute-done | bytes 786464 | tf_op jit(solution)/shard_map/ppermute | solution.py:252
  132.9 0.0 collective-permute-done.2.refs_3_
  132.9 7.7 %residual.3 = (bf16[768,2048]{1,0:T(8,128)(2,1)}, f32[256,2048]{1,0:T(8,128)}) custom-call(s32[4]{0:T(128)} %pad_add_fusion.order, bf16[192,2048]{1,0:T(8,128)(2,1)} %refs_0_.3, bf16[192,2048]{1,0:T(8,128)(2,1)} %collective-permute-done.refs_1_, bf16[192,2048]{1,0:T(8,128)(2,1)} %collective-permute-done.1.refs_2_, ...), custom_call_target="tpu_custom_call" | custom-call | flops 2415919104 | bytes 6291456 | tf_op jit(solution)/shard_map/residual/pallas_call | solution.py:181
  140.6 12.7 %covariance.3.refs_1_ = f32[2048,4096]{1,0:T(8,128)} custom-call(s32[2]{0:T(128)} %pad_add_fusion.2.where, bf16[768,2048]{1,0:T(8,128)(2,1)} %get-tuple-element.11.rows, bf16[768,1024]{1,0:T(8,128)(2,1)} %residual.5.refs_0_, bf16[768,1024]{1,0:T(8,128)(2,1)} %collective-permute-done.17.refs_1_), custom_call_target="tpu_custom_call" | custom-call | flops 6442450944 | bytes 16777216 | tf_op jit(solution)/shard_map/covariance/pallas_call | solution.py:221
  153.3 7.9 %covariance.4.refs_1_ = f32[2048,4096]{1,0:T(8,128)} custom-call(s32[1]{0:T(128)} %bitcast.9.where, bf16[768,2048]{1,0:T(8,128)(2,1)} %get-tuple-element.11.rows, bf16[768,1024]{1,0:T(8,128)(2,1)} %residual.4.refs_0_, f32[2048,4096]{1,0:T(8,128)} %covariance.3.refs_1_), custom_call_target="tpu_custom_call", output_to_operand_aliasing={{}: (3, {})} | custom-call | flops 3221225472 | bytes 8388608 | tf_op jit(solution)/shard_map/covariance/pallas_call | solution.py:221
  161.2 0.0 collective-permute-done.11.refs_0_
  161.2 7.9 %covariance.5 = f32[2048,4096]{1,0:T(8,128)} custom-call(s32[1]{0:T(128)} %bitcast.4.where, bf16[768,2048]{1,0:T(8,128)(2,1)} %get-tuple-element.11.rows, bf16[768,1024]{1,0:T(8,128)(2,1)} %collective-permute-done.11.refs_0_, f32[2048,4096]{1,0:T(8,128)} %covariance.4.refs_1_), custom_call_target="tpu_custom_call", output_to_operand_aliasing={{}: (3, {})} | custom-call | flops 3221225472 | bytes 8388608 | tf_op jit(solution)/shard_map/covariance/pallas_call | solution.py:221
  (7 shorter events, 0.0 us)
Async XLA Ops:
  2.5 26.4 %collective-permute-start.12 = (bf16[192,1024]{1,0:T(8,128)(2,1)S(1)}, bf16[192,1024]{1,0:T(8,128)(2,1)S(1)}, u32[]{:S(2)}, u32[]{:S(2)}) collective-permute-start(bf16[192,1024]{1,0:T(8,128)(2,1)S(1)} %get-tuple-element.14), channel_id=1, source_target_pairs={{0,4},{1,5},{2,6},{3,7},{4,0},{5,1},{6,2},{7,3},{8,12},{9,13},{10,... | collective-permute-start | bytes 1179656 | tf_op jit(solution)/shard_map/ppermute | solution.py:252
  2.5 31.0 %collective-permute-start.3 = (bf16[192,256]{1,0:T(8,128)(2,1)}, bf16[192,256]{1,0:T(8,128)(2,1)}, u32[]{:S(2)}, u32[]{:S(2)}) collective-permute-start(bf16[192,256]{1,0:T(8,128)(2,1)} %refs_0_.2), channel_id=1, source_target_pairs={{0,8},{1,9},{2,10},{3,11},{4,12},{5,13},{6,14},{7,15},{8,0},{9,1},... | collective-permute-start | bytes 294920 | tf_op jit(solution)/shard_map/ppermute | solution.py:252
  4.4 35.5 %collective-permute-start.4 = (bf16[192,256]{1,0:T(8,128)(2,1)}, bf16[192,256]{1,0:T(8,128)(2,1)}, u32[]{:S(2)}, u32[]{:S(2)}) collective-permute-start(bf16[192,256]{1,0:T(8,128)(2,1)} %refs_0_.2), channel_id=1, source_target_pairs={{0,16},{1,17},{2,18},{3,19},{4,20},{5,21},{6,22},{7,23},{8,24},{9,... | collective-permute-start | bytes 294920 | tf_op jit(solution)/shard_map/ppermute | solution.py:252
  5.9 38.5 %collective-permute-start.5 = (bf16[192,256]{1,0:T(8,128)(2,1)}, bf16[192,256]{1,0:T(8,128)(2,1)}, u32[]{:S(2)}, u32[]{:S(2)}) collective-permute-start(bf16[192,256]{1,0:T(8,128)(2,1)} %refs_0_.2), channel_id=1, source_target_pairs={{0,24},{1,25},{2,26},{3,27},{4,28},{5,29},{6,30},{7,31},{8,16},{9,... | collective-permute-start | bytes 294920 | tf_op jit(solution)/shard_map/ppermute | solution.py:252
  6.0 63.6 %collective-permute-start.6 = (bf16[192,1024]{1,0:T(8,128)(2,1)}, bf16[192,1024]{1,0:T(8,128)(2,1)}, u32[]{:S(2)}, u32[]{:S(2)}) collective-permute-start(bf16[192,1024]{1,0:T(8,128)(2,1)} %get-tuple-element.15), channel_id=1, source_target_pairs={{0,4},{1,5},{2,6},{3,7},{4,0},{5,1},{6,2},{7,3},{8,12},{9,13},{10,... | collective-permute-start | bytes 1179656 | tf_op jit(solution)/shard_map/ppermute | solution.py:252
  29.8 29.0 %collective-permute-start.13 = (bf16[192,1024]{1,0:T(8,128)(2,1)}, bf16[192,1024]{1,0:T(8,128)(2,1)}, u32[]{:S(2)}, u32[]{:S(2)}) collective-permute-start(bf16[192,1024]{1,0:T(8,128)(2,1)} %get-tuple-element.13), channel_id=1, source_target_pairs={{0,0},{1,1},{2,10},{3,11},{4,20},{5,21},{6,30},{7,31},{8,2},{9,3},... | collective-permute-start | bytes 1179656 | tf_op jit(solution)/shard_map/ppermute | solution.py:252
  33.6 25.3 %collective-permute-start.14 = (bf16[192,1024]{1,0:T(8,128)(2,1)}, bf16[192,1024]{1,0:T(8,128)(2,1)}, u32[]{:S(2)}, u32[]{:S(2)}) collective-permute-start(bf16[192,1024]{1,0:T(8,128)(2,1)} %get-tuple-element.13), channel_id=1, source_target_pairs={{0,2},{1,3},{2,8},{3,9},{4,22},{5,23},{6,28},{7,29},{8,0},{9,1},{1... | collective-permute-start | bytes 1179656 | tf_op jit(solution)/shard_map/ppermute | solution.py:252
  39.9 19.0 %collective-permute-start.15 = (bf16[192,1024]{1,0:T(8,128)(2,1)}, bf16[192,1024]{1,0:T(8,128)(2,1)}, u32[]{:S(2)}, u32[]{:S(2)}) collective-permute-start(bf16[192,1024]{1,0:T(8,128)(2,1)} %get-tuple-element.12), channel_id=1, source_target_pairs={{0,16},{1,17},{2,26},{3,27},{4,4},{5,5},{6,14},{7,15},{8,18},{9,19... | collective-permute-start | bytes 1179656 | tf_op jit(solution)/shard_map/ppermute | solution.py:252
  44.4 20.1 %collective-permute-start.16 = (bf16[192,1024]{1,0:T(8,128)(2,1)}, bf16[192,1024]{1,0:T(8,128)(2,1)}, u32[]{:S(2)}, u32[]{:S(2)}) collective-permute-start(bf16[192,1024]{1,0:T(8,128)(2,1)} %get-tuple-element.12), channel_id=1, source_target_pairs={{0,18},{1,19},{2,24},{3,25},{4,6},{5,7},{6,12},{7,13},{8,16},{9,17... | collective-permute-start | bytes 1179656 | tf_op jit(solution)/shard_map/ppermute | solution.py:252
  69.6 71.0 %collective-permute-start.17 = (bf16[768,1024]{1,0:T(8,128)(2,1)}, bf16[768,1024]{1,0:T(8,128)(2,1)}, u32[]{:S(2)}, u32[]{:S(2)}) collective-permute-start(bf16[768,1024]{1,0:T(8,128)(2,1)} %residual.5.refs_0_), channel_id=1, source_target_pairs={{0,1},{1,0},{2,3},{3,2},{4,5},{5,4},{6,7},{7,6},{8,9},{9,8},{10,11... | collective-permute-start | bytes 4718600 | tf_op jit(solution)/shard_map/ppermute | solution.py:252
  70.8 13.9 %collective-permute-start.10 = (bf16[192,1024]{1,0:T(8,128)(2,1)S(1)}, bf16[192,1024]{1,0:T(8,128)(2,1)S(1)}, u32[]{:S(2)}, u32[]{:S(2)}) collective-permute-start(bf16[192,1024]{1,0:T(8,128)(2,1)S(1)} %get-tuple-element.16), channel_id=1, source_target_pairs={{0,18},{1,19},{2,24},{3,25},{4,6},{5,7},{6,12},{7,13},{8,16},{9,17... | collective-permute-start | bytes 1179656 | tf_op jit(solution)/shard_map/ppermute | solution.py:252
  75.2 21.6 %collective-permute-start.7 = (bf16[192,1024]{1,0:T(8,128)(2,1)S(1)}, bf16[192,1024]{1,0:T(8,128)(2,1)S(1)}, u32[]{:S(2)}, u32[]{:S(2)}) collective-permute-start(bf16[192,1024]{1,0:T(8,128)(2,1)S(1)} %get-tuple-element.17), channel_id=1, source_target_pairs={{0,0},{1,1},{2,10},{3,11},{4,20},{5,21},{6,30},{7,31},{8,2},{9,3},... | collective-permute-start | bytes 1179656 | tf_op jit(solution)/shard_map/ppermute | solution.py:252
  78.7 19.7 %collective-permute-start.8 = (bf16[192,1024]{1,0:T(8,128)(2,1)S(1)}, bf16[192,1024]{1,0:T(8,128)(2,1)S(1)}, u32[]{:S(2)}, u32[]{:S(2)}) collective-permute-start(bf16[192,1024]{1,0:T(8,128)(2,1)S(1)} %get-tuple-element.17), channel_id=1, source_target_pairs={{0,2},{1,3},{2,8},{3,9},{4,22},{5,23},{6,28},{7,29},{8,0},{9,1},{1... | collective-permute-start | bytes 1179656 | tf_op jit(solution)/shard_map/ppermute | solution.py:252
  80.6 18.5 %collective-permute-start.9 = (bf16[192,1024]{1,0:T(8,128)(2,1)S(1)}, bf16[192,1024]{1,0:T(8,128)(2,1)}, u32[]{:S(2)}, u32[]{:S(2)}) collective-permute-start(bf16[192,1024]{1,0:T(8,128)(2,1)S(1)} %get-tuple-element.16), channel_id=1, source_target_pairs={{0,16},{1,17},{2,26},{3,27},{4,4},{5,5},{6,14},{7,15},{8,18},{9,19... | collective-permute-start | bytes 1179656 | tf_op jit(solution)/shard_map/ppermute | solution.py:252
  84.7 13.6 %copy-start = (bf16[192,1024]{1,0:T(8,128)(2,1)}, bf16[192,1024]{1,0:T(8,128)(2,1)S(1)}, u32[]{:S(2)}) copy-start(bf16[192,1024]{1,0:T(8,128)(2,1)S(1)} %collective-permute-done.10.refs_3_) | copy-start | bytes 1179652
  84.7 26.0 %collective-permute-start = (bf16[192,2048]{1,0:T(8,128)(2,1)}, bf16[192,2048]{1,0:T(8,128)(2,1)}, u32[]{:S(2)}, u32[]{:S(2)}) collective-permute-start(bf16[192,2048]{1,0:T(8,128)(2,1)} %refs_0_.3), channel_id=1, source_target_pairs={{0,8},{1,9},{2,10},{3,11},{4,12},{5,13},{6,14},{7,15},{8,0},{9,1},... | collective-permute-start | bytes 2359304 | tf_op jit(solution)/shard_map/ppermute | solution.py:252
  96.8 1.6 copy-start.1
  96.8 36.1 %collective-permute-start.1 = (bf16[192,2048]{1,0:T(8,128)(2,1)}, bf16[192,2048]{1,0:T(8,128)(2,1)}, u32[]{:S(2)}, u32[]{:S(2)}) collective-permute-start(bf16[192,2048]{1,0:T(8,128)(2,1)} %refs_0_.3), channel_id=1, source_target_pairs={{0,16},{1,17},{2,18},{3,19},{4,20},{5,21},{6,22},{7,23},{8,24},{9,... | collective-permute-start | bytes 2359304 | tf_op jit(solution)/shard_map/ppermute | solution.py:252
  98.3 0.8 copy-start.2
  98.3 34.6 %collective-permute-start.2 = (bf16[192,2048]{1,0:T(8,128)(2,1)}, bf16[192,2048]{1,0:T(8,128)(2,1)}, u32[]{:S(2)}, u32[]{:S(2)}) collective-permute-start(bf16[192,2048]{1,0:T(8,128)(2,1)} %refs_0_.3), channel_id=1, source_target_pairs={{0,24},{1,25},{2,26},{3,27},{4,28},{5,29},{6,30},{7,31},{8,16},{9,... | collective-permute-start | bytes 2359304 | tf_op jit(solution)/shard_map/ppermute | solution.py:252
  104.3 56.9 %collective-permute-start.11 = (bf16[768,1024]{1,0:T(8,128)(2,1)}, bf16[768,1024]{1,0:T(8,128)(2,1)}, u32[]{:S(2)}, u32[]{:S(2)}) collective-permute-start(bf16[768,1024]{1,0:T(8,128)(2,1)} %residual.4.refs_0_), channel_id=1, source_target_pairs={{0,1},{1,0},{2,3},{3,2},{4,5},{5,4},{6,7},{7,6},{8,9},{9,8},{10,11... | collective-permute-start | bytes 4718600 | tf_op jit(solution)/shard_map/ppermute | solution.py:252
where the time goes:
time: 170 us; the launch traced here: 169 us
  waiting for transfers between devices  65 us (38%)
  Pallas kernels  59.2 us (35%)
  starting transfers between devices  37.5 us (22%)
  other arithmetic  3.94 us (2%)
  local copies, waits for them, and re-layouts  2.61 us (2%)
    ppermute x18, waiting for transfers between devices, move(): return lax.ppermute(x, AXES, pairs)  65 us
    ppermute x18, starting transfers between devices, move(): return lax.ppermute(x, AXES, pairs)  37.5 us
    pallas_call x3, Pallas kernels, covariance(): pl.pallas_call(functools.partial(covariance_kernel, 1.0 / days, count), g...  28.5 us
    pallas_call x3, Pallas kernels, residuals(): pl.pallas_call(functools.partial(residual_kernel, n, halves, with_loading...  18.2 us
    pallas_call x1, Pallas kernels, invert(): pl.pallas_call(functools.partial(invert_kernel, n), in_specs=[pl.BlockSpe...  12.6 us
  transfers between devices with their start and end apart: 18, of which 6 were waited for; matrix products, arithmetic and copies ran while one was open for 2% of the time, Pallas kernels for 30%

commit v1 on v0

--- a/solution.py
+++ b/solution.py
@@ -126,31 +126,15 @@
     )(order, *pieces)
 
 
-def residual_kernel(n, halves, with_loadings, order, *refs):
-    tiles = pl.num_programs(0)
-    count = n + 1 if halves else n
-    pieces = refs[:count]
+def residual_kernel(slots, depth, with_loadings, order, *refs):
+    count = len(slots)
     high, low, factors = refs[count : count + 3]
     outs = refs[count + 3 : -1]
     y = refs[-1]
-    depth = pieces[0].shape[0]
-
-    def put(j, ref):
-        y[pl.ds(pl.multiple_of(order[j] * depth, depth), depth), :] = ref[...]
-
-    for j in range(n - 1 if halves else n):
-        put(j, pieces[j])
-    if halves:
-        left = pl.program_id(0) < tiles // 2
-
-        @pl.when(left)
-        def _():
-            put(n - 1, pieces[n - 1])
-
-        @pl.when(jnp.logical_not(left))
-        def _():
-            put(n - 1, pieces[n])
-
+    for (j, offset), ref in zip(slots, refs[:count]):
+        rows = ref.shape[0]
+        at = pl.multiple_of(order[j] * depth, depth) + offset
+        y[pl.ds(pl.multiple_of(at, rows), rows), :] = ref[...]
     loadings = dot(high[...], y[...]) + dot(low[...], y[...])
     fitted = dot(factors[...], loadings.astype(BF))
     outs[0][...] = (y[...].astype(F32) - fitted).astype(BF)
@@ -158,31 +142,22 @@
         outs[1][...] = loadings
 
 
-def residuals(order, pieces, high, low, factors, width, with_loadings, halves=False, tile=512):
-    n = len(pieces) - 1 if halves else len(pieces)
-    depth = pieces[0].shape[0]
+def residuals(order, pieces, slots, high, low, factors, width, with_loadings, tile=1024):
     size, days = high.shape
-    tile = min(tile, width // 2 if halves else width)
-    tiles = width // tile
-    spec = pl.BlockSpec((depth, tile), lambda i, order: (0, i))
-    specs = [spec] * n
-    if halves:
-        half = tiles // 2
-        specs = specs[:-1] + [
-            pl.BlockSpec((depth, tile), lambda i, order: (0, jnp.minimum(i, half - 1))),
-            pl.BlockSpec((depth, tile), lambda i, order: (0, jnp.maximum(i - half, 0))),
-        ]
+    depth = days // order.shape[0]
+    tile = min(tile, width)
     whole = lambda shape: pl.BlockSpec(shape, lambda i, order: (0, 0))
+    specs = [pl.BlockSpec((p.shape[0], tile), lambda i, order: (0, i)) for p in pieces]
     out_specs = [pl.BlockSpec((days, tile), lambda i, order: (0, i))]
     out_shape = [jax.ShapeDtypeStruct((days, width), BF)]
     if with_loadings:
         out_specs.append(pl.BlockSpec((size, tile), lambda i, order: (0, i)))
         out_shape.append(jax.ShapeDtypeStruct((size, width), F32))
     return pl.pallas_call(
-        functools.partial(residual_kernel, n, halves, with_loadings),
+        functools.partial(residual_kernel, slots, depth, with_loadings),
         grid_spec=pltpu.PrefetchScalarGridSpec(
             num_scalar_prefetch=1,
-            grid=(tiles,),
+            grid=(width // tile,),
             in_specs=specs + [whole((size, days))] * 2 + [whole((days, size))],
             out_specs=out_specs,
             scratch_shapes=[pltpu.VMEM((days, tile), BF)],
@@ -234,6 +209,10 @@
     )(jnp.stack([lax.div(s, tile) for s in starts]).astype(jnp.int32), *args)
 
 
+def relayed(nd):
+    return nd == 4
+
+
 def per_device(nd, na, factors, returns):
     reps = na // nd
     depth, width = returns.shape
@@ -267,7 +246,17 @@
         return move(x, lambda d, q, c: (shift(d, j), q, c))
 
     factor_pieces = [factors] + [plane(factors, j) for j in range(1, nd)]
-    row_pieces = [returns] + [plane(returns, j) for j in range(1, nd)]
+    slots = [(j, 0) for j in range(nd)]
+    if relayed(nd):
+        half = depth // 2
+        one, two = plane(returns, 1), plane(returns, 2)
+        upper = one[:half]
+        lower = two[half:]
+        row_pieces = [returns, one, two, plane(upper, 2), plane(lower, 1)]
+        row_slots = slots[:3] + [(3, 0), (3, half)]
+    else:
+        row_pieces = [returns] + [plane(returns, j) for j in range(1, nd)]
+        row_slots = slots
 
     sizes = [width * s // sum(CHUNKS) for s in CHUNKS]
     starts = [sum(sizes[:i]) for i in range(len(sizes))]
@@ -289,12 +278,12 @@
         chunk_pieces.append(pieces)
 
     full, high, low = invert(order, factor_pieces)
-    rows, loadings = residuals(order, row_pieces, high, low, full, width, True)
+    rows, loadings = residuals(order, row_pieces, row_slots, high, low, full, width, True)
 
     held = None
     total = reps * width
     for i, (start, pieces) in enumerate(zip(starts, chunk_pieces)):
-        (cols,) = residuals(col_order, pieces, high, low, full, sizes[i], False)
+        (cols,) = residuals(col_order, pieces, slots, high, low, full, sizes[i], False)
         parts, at = [], []
         for s in range(reps):
             parts.append(cols if s == 0 else move(cols, lambda d, q, c: (d, q, (c - s) % reps)))

time: 170 us -> 172 us (1.012)
  local copies, waits for them, and re-layouts: 2.61 us -> 5.46 us
  starting transfers between devices: 37.5 us -> 40.2 us
  waiting for transfers between devices: 65 us -> 62.7 us
    ppermute x18 -> x19, starting transfers between devices: 37.5 us -> 40.2 us  [move(): return lax.ppermute(x, AXES, pairs)]
    ppermute x18 -> x19, waiting for transfers between devices: 65 us -> 62.7 us  [move(): return lax.ppermute(x, AXES, pairs)]
    slice x0 -> x2, local copies, waits for them, and re-layouts: none -> 2.04 us  [the longest x1 1.02 us: per_device(): upper = one[:half]]
  transfers between devices with their start and end apart: 18 -> 19, of which waited for: 6 -> 6; matrix products, arithmetic and copies ran while one was open for 2% -> 4% of each run, Pallas kernels for 30% -> 29%
where the time goes in v1:
time: 172 us; the launch traced here: 171 us
  waiting for transfers between devices  62.7 us (36%)
  Pallas kernels  58 us (34%)
  starting transfers between devices  40.2 us (23%)
  local copies, waits for them, and re-layouts  5.46 us (3%)
  other arithmetic  3.95 us (2%)
    ppermute x19, waiting for transfers between devices, move(): return lax.ppermute(x, AXES, pairs)  62.7 us
    ppermute x19, starting transfers between devices, move(): return lax.ppermute(x, AXES, pairs)  40.2 us
    pallas_call x3, Pallas kernels, covariance(): pl.pallas_call(functools.partial(covariance_kernel, 1.0 / days, count), g...  28.5 us
    pallas_call x3, Pallas kernels, residuals(): pl.pallas_call(functools.partial(residual_kernel, slots, depth, with_load...  16.9 us
    pallas_call x1, Pallas kernels, invert(): pl.pallas_call(functools.partial(invert_kernel, n), in_specs=[pl.BlockSpe...  12.6 us
  transfers between devices with their start and end apart: 19, of which 6 were waited for; matrix products, arithmetic and copies ran while one was open for 4% of the time, Pallas kernels for 29%

profile of v1, /device:TPU:16, one launch (start us, length us, event | category | flops | bytes accessed | tf_op | source)
XLA Modules:
  0.0 171.1 jit_solution(10596959686870718413)
XLA Ops:
  0.6 1.9 %fusion = (bf16[192,1024]{1,0:T(8,128)(2,1)S(1)}, bf16[192,1024]{1,0:T(8,128)(2,1)}) fusion(bf16[192,2048]{1,0:T(8,128)(2,1)} %refs_0_.3), kind=kLoop, calls=%fused_computation.7 | loop fusion | bytes 1572864 | tf_op jit(solution)/shard_map/slice | solution.py:266
  2.5 0.0 collective-permute-start.13
  2.5 1.8 %collective-permute-start.4 = (bf16[192,256]{1,0:T(8,128)(2,1)}, bf16[192,256]{1,0:T(8,128)(2,1)}, u32[]{:S(2)}, u32[]{:S(2)}) collective-permute-start(bf16[192,256]{1,0:T(8,128)(2,1)} %refs_0_.2), channel_id=1, source_target_pairs={{0,8},{1,9},{2,10},{3,11},{4,12},{5,13},{6,14},{7,15},{8,0},{9,1},... | collective-permute-start | bytes 294920 | tf_op jit(solution)/shard_map/ppermute | solution.py:231
  4.4 1.5 collective-permute-start.5
  5.9 0.1 collective-permute-start.6
  6.0 2.9 %collective-permute-start.7 = (bf16[192,1024]{1,0:T(8,128)(2,1)}, bf16[192,1024]{1,0:T(8,128)(2,1)}, u32[]{:S(2)}, u32[]{:S(2)}) collective-permute-start(bf16[192,1024]{1,0:T(8,128)(2,1)} %get-tuple-element.15), channel_id=1, source_target_pairs={{0,4},{1,5},{2,6},{3,7},{4,0},{5,1},{6,2},{7,3},{8,12},{9,13},{10,... | collective-permute-start | bytes 1179656 | tf_op jit(solution)/shard_map/ppermute | solution.py:231
  9.0 0.6 pad_add_fusion.1.order
  9.6 0.6 pad_add_fusion.order
  10.2 18.7 %collective-permute-done.13 = bf16[192,1024]{1,0:T(8,128)(2,1)S(1)} collective-permute-done((bf16[192,1024]{1,0:T(8,128)(2,1)S(1)}, bf16[192,1024]{1,0:T(8,128)(2,1)S(1)}, u32[]{:S(2)}, u32[]{:S(2)}) %collective-permute-start.13) | collective-permute-done | bytes 393248 | tf_op jit(solution)/shard_map/ppermute | solution.py:231
  28.9 0.9 broadcast_select_fusion
  29.8 3.7 %collective-permute-start.14 = (bf16[192,1024]{1,0:T(8,128)(2,1)}, bf16[192,1024]{1,0:T(8,128)(2,1)}, u32[]{:S(2)}, u32[]{:S(2)}) collective-permute-start(bf16[192,1024]{1,0:T(8,128)(2,1)} %get-tuple-element.13), channel_id=1, source_target_pairs={{0,0},{1,1},{2,10},{3,11},{4,20},{5,21},{6,30},{7,31},{8,2},{9,3},... | collective-permute-start | bytes 1179656 | tf_op jit(solution)/shard_map/ppermute | solution.py:231
  33.6 6.3 %collective-permute-start.15 = (bf16[192,1024]{1,0:T(8,128)(2,1)}, bf16[192,1024]{1,0:T(8,128)(2,1)}, u32[]{:S(2)}, u32[]{:S(2)}) collective-permute-start(bf16[192,1024]{1,0:T(8,128)(2,1)} %get-tuple-element.13), channel_id=1, source_target_pairs={{0,2},{1,3},{2,8},{3,9},{4,22},{5,23},{6,28},{7,29},{8,0},{9,1},{1... | collective-permute-start | bytes 1179656 | tf_op jit(solution)/shard_map/ppermute | solution.py:231
  39.9 0.0 collective-permute-done.5.refs_2_
  39.9 4.5 %collective-permute-start.16 = (bf16[192,1024]{1,0:T(8,128)(2,1)}, bf16[192,1024]{1,0:T(8,128)(2,1)}, u32[]{:S(2)}, u32[]{:S(2)}) collective-permute-start(bf16[192,1024]{1,0:T(8,128)(2,1)} %get-tuple-element.12), channel_id=1, source_target_pairs={{0,16},{1,17},{2,26},{3,27},{4,4},{5,5},{6,14},{7,15},{8,18},{9,19... | collective-permute-start | bytes 1179656 | tf_op jit(solution)/shard_map/ppermute | solution.py:231
  44.4 1.9 %collective-permute-start.17 = (bf16[192,1024]{1,0:T(8,128)(2,1)}, bf16[192,1024]{1,0:T(8,128)(2,1)}, u32[]{:S(2)}, u32[]{:S(2)}) collective-permute-start(bf16[192,1024]{1,0:T(8,128)(2,1)} %get-tuple-element.12), channel_id=1, source_target_pairs={{0,18},{1,19},{2,24},{3,25},{4,6},{5,7},{6,12},{7,13},{8,16},{9,17... | collective-permute-start | bytes 1179656 | tf_op jit(solution)/shard_map/ppermute | solution.py:231
  46.3 12.6 %gram.1 = (bf16[768,256]{1,0:T(8,128)(2,1)}, bf16[256,768]{1,0:T(8,128)(2,1)}, bf16[256,768]{1,0:T(8,128)(2,1)}) custom-call(s32[4]{0:T(128)} %pad_add_fusion.order, bf16[192,256]{1,0:T(8,128)(2,1)} %refs_0_.2, bf16[192,256]{1,0:T(8,128)(2,1)} %collective-permute-done.4.refs_1_, bf16[192,256]{1,0:T(8,128)(2,1)} %collective-permute-done.5.refs_2_, ...), custom_call_target="tpu_custom_call" | custom-call | flops 20000000000 | bytes 1572864 | tf_op jit(solution)/shard_map/gram/pallas_call | solution.py:118
  58.9 0.0 collective-permute-done.14.refs_0_
  58.9 0.0 collective-permute-done.15.refs_1_
  58.9 5.5 %collective-permute-done.17.refs_3_ = bf16[192,1024]{1,0:T(8,128)(2,1)} collective-permute-done((bf16[192,1024]{1,0:T(8,128)(2,1)}, bf16[192,1024]{1,0:T(8,128)(2,1)}, u32[]{:S(2)}, u32[]{:S(2)}) %collective-permute-start.17) | collective-permute-done | bytes 393248 | tf_op jit(solution)/shard_map/ppermute | solution.py:231
  64.4 5.0 %residual.5.refs_0_ = bf16[768,1024]{1,0:T(8,128)(2,1)} custom-call(s32[4]{0:T(128)} %pad_add_fusion.1.order, bf16[192,1024]{1,0:T(8,128)(2,1)} %collective-permute-done.14.refs_0_, bf16[192,1024]{1,0:T(8,128)(2,1)} %collective-permute-done.15.refs_1_, bf16[192,1024]{1,0:T(8,128)(2,1)} %collective-permute-done.16.refs_2_, ...), custom_call_target="tpu_custom_call" | custom-call | flops 1207959552 | bytes 3145728 | tf_op jit(solution)/shard_map/residual/pallas_call | solution.py:156
  69.4 0.0 collective-permute-start.18
  69.4 0.0 collective-permute-done.7
  69.5 1.2 broadcast_select_fusion.2
  70.6 0.7 collective-permute-start.10
  71.3 5.6 %collective-permute-start.11 = (bf16[192,1024]{1,0:T(8,128)(2,1)S(1)}, bf16[192,1024]{1,0:T(8,128)(2,1)S(1)}, u32[]{:S(2)}, u32[]{:S(2)}) collective-permute-start(bf16[192,1024]{1,0:T(8,128)(2,1)S(1)} %get-tuple-element.16), channel_id=1, source_target_pairs={{0,18},{1,19},{2,24},{3,25},{4,6},{5,7},{6,12},{7,13},{8,16},{9,17... | collective-permute-start | bytes 1179656 | tf_op jit(solution)/shard_map/ppermute | solution.py:231
  77.0 1.5 collective-permute-start
  78.5 1.5 collective-permute-start.1
  80.0 0.0 collective-permute-done.10.refs_2_
  80.0 2.4 %collective-permute-start.8 = (bf16[192,1024]{1,0:T(8,128)(2,1)S(1)}, bf16[192,1024]{1,0:T(8,128)(2,1)S(1)}, u32[]{:S(2)}, u32[]{:S(2)}) collective-permute-start(bf16[192,1024]{1,0:T(8,128)(2,1)S(1)} %get-tuple-element.17), channel_id=1, source_target_pairs={{0,0},{1,1},{2,10},{3,11},{4,20},{5,21},{6,30},{7,31},{8,2},{9,3},... | collective-permute-start | bytes 1179656 | tf_op jit(solution)/shard_map/ppermute | solution.py:231
  82.4 5.9 %collective-permute-done.11.refs_3_ = bf16[192,1024]{1,0:T(8,128)(2,1)S(1)} collective-permute-done((bf16[192,1024]{1,0:T(8,128)(2,1)S(1)}, bf16[192,1024]{1,0:T(8,128)(2,1)S(1)}, u32[]{:S(2)}, u32[]{:S(2)}) %collective-permute-start.11) | collective-permute-done | bytes 393248 | tf_op jit(solution)/shard_map/ppermute | solution.py:231
  88.4 4.0 %collective-permute-start.9 = (bf16[192,1024]{1,0:T(8,128)(2,1)S(1)}, bf16[192,1024]{1,0:T(8,128)(2,1)}, u32[]{:S(2)}, u32[]{:S(2)}) collective-permute-start(bf16[192,1024]{1,0:T(8,128)(2,1)S(1)} %get-tuple-element.17), channel_id=1, source_target_pairs={{0,2},{1,3},{2,8},{3,9},{4,22},{5,23},{6,28},{7,29},{8,0},{9,1},{1... | collective-permute-start | bytes 1179656 | tf_op jit(solution)/shard_map/ppermute | solution.py:231
  92.3 22.6 %collective-permute-done.8.refs_0_ = bf16[192,1024]{1,0:T(8,128)(2,1)S(1)} collective-permute-done((bf16[192,1024]{1,0:T(8,128)(2,1)S(1)}, bf16[192,1024]{1,0:T(8,128)(2,1)S(1)}, u32[]{:S(2)}, u32[]{:S(2)}) %collective-permute-start.8) | collective-permute-done | bytes 393248 | tf_op jit(solution)/shard_map/ppermute | solution.py:231
  114.9 0.7 copy-done.3
  115.7 5.0 %residual.4.refs_0_ = bf16[768,1024]{1,0:T(8,128)(2,1)} custom-call(s32[4]{0:T(128)} %pad_add_fusion.1.order, bf16[192,1024]{1,0:T(8,128)(2,1)} %copy-done.3, bf16[192,1024]{1,0:T(8,128)(2,1)} %collective-permute-done.9.refs_1_, bf16[192,1024]{1,0:T(8,128)(2,1)} %copy-done.1, bf16[192,1024]{1,0:T(8,128)(2,1)} %copy-done.2, ...), custom_call_target="tpu_custom_call" | custom-call | flops 1207959552 | bytes 3145728 | tf_op jit(solution)/shard_map/residual/pallas_call | solution.py:156
  120.7 0.0 collective-permute-start.12
  120.7 0.0 collective-permute-done.refs_1_
  120.7 1.0 slice.16
  121.7 1.6 collective-permute-start.2
  123.3 1.0 slice.17
  124.4 0.1 collective-permute-start.3
  124.5 0.6 pad_add_fusion.2.where
  125.1 8.2 %collective-permute-done.2.refs_3_ = bf16[96,2048]{1,0:T(8,128)(2,1)S(1)} collective-permute-done((bf16[96,2048]{1,0:T(8,128)(2,1)S(1)}, bf16[96,2048]{1,0:T(8,128)(2,1)S(1)}, u32[]{:S(2)}, u32[]{:S(2)}) %collective-permute-start.2) | collective-permute-done | bytes 393248 | tf_op jit(solution)/shard_map/ppermute | solution.py:231
  133.3 0.7 copy-done
  134.1 1.7 collective-permute-done.3.refs_4_
  135.8 6.8 %residual.3 = (bf16[768,2048]{1,0:T(8,128)(2,1)}, f32[256,2048]{1,0:T(8,128)}) custom-call(s32[4]{0:T(128)} %pad_add_fusion.order, bf16[192,2048]{1,0:T(8,128)(2,1)} %refs_0_.3, bf16[192,2048]{1,0:T(8,128)(2,1)} %collective-permute-done.refs_1_, bf16[192,2048]{1,0:T(8,128)(2,1)} %collective-permute-done.1.refs_2_, bf16[96,2048]{1,0:T(8,128)(2,1)} %copy-done, ...), custom_call_target="tpu_custom_call" | custom-call | flops 2415919104 | bytes 6291456 | tf_op jit(solution)/shard_map/residual/pallas_call | solution.py:156
  142.6 12.7 %covariance.3.refs_1_ = f32[2048,4096]{1,0:T(8,128)} custom-call(s32[2]{0:T(128)} %pad_add_fusion.2.where, bf16[768,2048]{1,0:T(8,128)(2,1)} %get-tuple-element.11.rows, bf16[768,1024]{1,0:T(8,128)(2,1)} %residual.5.refs_0_, bf16[768,1024]{1,0:T(8,128)(2,1)} %collective-permute-done.18.refs_1_), custom_call_target="tpu_custom_call" | custom-call | flops 6442450944 | bytes 16777216 | tf_op jit(solution)/shard_map/covariance/pallas_call | solution.py:196
  155.3 7.9 %covariance.4.refs_1_ = f32[2048,4096]{1,0:T(8,128)} custom-call(s32[1]{0:T(128)} %bitcast.9.where, bf16[768,2048]{1,0:T(8,128)(2,1)} %get-tuple-element.11.rows, bf16[768,1024]{1,0:T(8,128)(2,1)} %residual.4.refs_0_, f32[2048,4096]{1,0:T(8,128)} %covariance.3.refs_1_), custom_call_target="tpu_custom_call", output_to_operand_aliasing={{}: (3, {})} | custom-call | flops 3221225472 | bytes 8388608 | tf_op jit(solution)/shard_map/covariance/pallas_call | solution.py:196
  163.2 7.9 %covariance.5 = f32[2048,4096]{1,0:T(8,128)} custom-call(s32[1]{0:T(128)} %bitcast.4.where, bf16[768,2048]{1,0:T(8,128)(2,1)} %get-tuple-element.11.rows, bf16[768,1024]{1,0:T(8,128)(2,1)} %collective-permute-done.12.refs_0_, f32[2048,4096]{1,0:T(8,128)} %covariance.4.refs_1_), custom_call_target="tpu_custom_call", output_to_operand_aliasing={{}: (3, {})} | custom-call | flops 3221225472 | bytes 8388608 | tf_op jit(solution)/shard_map/covariance/pallas_call | solution.py:196
  (13 shorter events, 0.0 us)
Async XLA Ops:
  2.5 26.4 %collective-permute-start.13 = (bf16[192,1024]{1,0:T(8,128)(2,1)S(1)}, bf16[192,1024]{1,0:T(8,128)(2,1)S(1)}, u32[]{:S(2)}, u32[]{:S(2)}) collective-permute-start(bf16[192,1024]{1,0:T(8,128)(2,1)S(1)} %get-tuple-element.14), channel_id=1, source_target_pairs={{0,4},{1,5},{2,6},{3,7},{4,0},{5,1},{6,2},{7,3},{8,12},{9,13},{10,... | collective-permute-start | bytes 1179656 | tf_op jit(solution)/shard_map/ppermute | solution.py:231
  2.5 31.0 %collective-permute-start.4 = (bf16[192,256]{1,0:T(8,128)(2,1)}, bf16[192,256]{1,0:T(8,128)(2,1)}, u32[]{:S(2)}, u32[]{:S(2)}) collective-permute-start(bf16[192,256]{1,0:T(8,128)(2,1)} %refs_0_.2), channel_id=1, source_target_pairs={{0,8},{1,9},{2,10},{3,11},{4,12},{5,13},{6,14},{7,15},{8,0},{9,1},... | collective-permute-start | bytes 294920 | tf_op jit(solution)/shard_map/ppermute | solution.py:231
  4.4 35.5 %collective-permute-start.5 = (bf16[192,256]{1,0:T(8,128)(2,1)}, bf16[192,256]{1,0:T(8,128)(2,1)}, u32[]{:S(2)}, u32[]{:S(2)}) collective-permute-start(bf16[192,256]{1,0:T(8,128)(2,1)} %refs_0_.2), channel_id=1, source_target_pairs={{0,16},{1,17},{2,18},{3,19},{4,20},{5,21},{6,22},{7,23},{8,24},{9,... | collective-permute-start | bytes 294920 | tf_op jit(solution)/shard_map/ppermute | solution.py:231
  5.9 38.5 %collective-permute-start.6 = (bf16[192,256]{1,0:T(8,128)(2,1)}, bf16[192,256]{1,0:T(8,128)(2,1)}, u32[]{:S(2)}, u32[]{:S(2)}) collective-permute-start(bf16[192,256]{1,0:T(8,128)(2,1)} %refs_0_.2), channel_id=1, source_target_pairs={{0,24},{1,25},{2,26},{3,27},{4,28},{5,29},{6,30},{7,31},{8,16},{9,... | collective-permute-start | bytes 294920 | tf_op jit(solution)/shard_map/ppermute | solution.py:231
  6.0 63.4 %collective-permute-start.7 = (bf16[192,1024]{1,0:T(8,128)(2,1)}, bf16[192,1024]{1,0:T(8,128)(2,1)}, u32[]{:S(2)}, u32[]{:S(2)}) collective-permute-start(bf16[192,1024]{1,0:T(8,128)(2,1)} %get-tuple-element.15), channel_id=1, source_target_pairs={{0,4},{1,5},{2,6},{3,7},{4,0},{5,1},{6,2},{7,3},{8,12},{9,13},{10,... | collective-permute-start | bytes 1179656 | tf_op jit(solution)/shard_map/ppermute | solution.py:231
  29.8 29.0 %collective-permute-start.14 = (bf16[192,1024]{1,0:T(8,128)(2,1)}, bf16[192,1024]{1,0:T(8,128)(2,1)}, u32[]{:S(2)}, u32[]{:S(2)}) collective-permute-start(bf16[192,1024]{1,0:T(8,128)(2,1)} %get-tuple-element.13), channel_id=1, source_target_pairs={{0,0},{1,1},{2,10},{3,11},{4,20},{5,21},{6,30},{7,31},{8,2},{9,3},... | collective-permute-start | bytes 1179656 | tf_op jit(solution)/shard_map/ppermute | solution.py:231
  33.6 25.3 %collective-permute-start.15 = (bf16[192,1024]{1,0:T(8,128)(2,1)}, bf16[192,1024]{1,0:T(8,128)(2,1)}, u32[]{:S(2)}, u32[]{:S(2)}) collective-permute-start(bf16[192,1024]{1,0:T(8,128)(2,1)} %get-tuple-element.13), channel_id=1, source_target_pairs={{0,2},{1,3},{2,8},{3,9},{4,22},{5,23},{6,28},{7,29},{8,0},{9,1},{1... | collective-permute-start | bytes 1179656 | tf_op jit(solution)/shard_map/ppermute | solution.py:231
  39.9 19.0 %collective-permute-start.16 = (bf16[192,1024]{1,0:T(8,128)(2,1)}, bf16[192,1024]{1,0:T(8,128)(2,1)}, u32[]{:S(2)}, u32[]{:S(2)}) collective-permute-start(bf16[192,1024]{1,0:T(8,128)(2,1)} %get-tuple-element.12), channel_id=1, source_target_pairs={{0,16},{1,17},{2,26},{3,27},{4,4},{5,5},{6,14},{7,15},{8,18},{9,19... | collective-permute-start | bytes 1179656 | tf_op jit(solution)/shard_map/ppermute | solution.py:231
  44.4 20.0 %collective-permute-start.17 = (bf16[192,1024]{1,0:T(8,128)(2,1)}, bf16[192,1024]{1,0:T(8,128)(2,1)}, u32[]{:S(2)}, u32[]{:S(2)}) collective-permute-start(bf16[192,1024]{1,0:T(8,128)(2,1)} %get-tuple-element.12), channel_id=1, source_target_pairs={{0,18},{1,19},{2,24},{3,25},{4,6},{5,7},{6,12},{7,13},{8,16},{9,17... | collective-permute-start | bytes 1179656 | tf_op jit(solution)/shard_map/ppermute | solution.py:231
  69.4 73.2 %collective-permute-start.18 = (bf16[768,1024]{1,0:T(8,128)(2,1)}, bf16[768,1024]{1,0:T(8,128)(2,1)}, u32[]{:S(2)}, u32[]{:S(2)}) collective-permute-start(bf16[768,1024]{1,0:T(8,128)(2,1)} %residual.5.refs_0_), channel_id=1, source_target_pairs={{0,1},{1,0},{2,3},{3,2},{4,5},{5,4},{6,7},{7,6},{8,9},{9,8},{10,11... | collective-permute-start | bytes 4718600 | tf_op jit(solution)/shard_map/ppermute | solution.py:231
  70.6 9.4 %collective-permute-start.10 = (bf16[192,1024]{1,0:T(8,128)(2,1)S(1)}, bf16[192,1024]{1,0:T(8,128)(2,1)S(1)}, u32[]{:S(2)}, u32[]{:S(2)}) collective-permute-start(bf16[192,1024]{1,0:T(8,128)(2,1)S(1)} %get-tuple-element.16), channel_id=1, source_target_pairs={{0,16},{1,17},{2,26},{3,27},{4,4},{5,5},{6,14},{7,15},{8,18},{9,19... | collective-permute-start | bytes 1179656 | tf_op jit(solution)/shard_map/ppermute | solution.py:231
  71.3 17.0 %collective-permute-start.11 = (bf16[192,1024]{1,0:T(8,128)(2,1)S(1)}, bf16[192,1024]{1,0:T(8,128)(2,1)S(1)}, u32[]{:S(2)}, u32[]{:S(2)}) collective-permute-start(bf16[192,1024]{1,0:T(8,128)(2,1)S(1)} %get-tuple-element.16), channel_id=1, source_target_pairs={{0,18},{1,19},{2,24},{3,25},{4,6},{5,7},{6,12},{7,13},{8,16},{9,17... | collective-permute-start | bytes 1179656 | tf_op jit(solution)/shard_map/ppermute | solution.py:231
  77.0 43.8 %collective-permute-start = (bf16[192,2048]{1,0:T(8,128)(2,1)}, bf16[192,2048]{1,0:T(8,128)(2,1)}, u32[]{:S(2)}, u32[]{:S(2)}) collective-permute-start(bf16[192,2048]{1,0:T(8,128)(2,1)} %refs_0_.3), channel_id=1, source_target_pairs={{0,8},{1,9},{2,10},{3,11},{4,12},{5,13},{6,14},{7,15},{8,0},{9,1},... | collective-permute-start | bytes 2359304 | tf_op jit(solution)/shard_map/ppermute | solution.py:231
  78.5 44.9 %collective-permute-start.1 = (bf16[192,2048]{1,0:T(8,128)(2,1)}, bf16[192,2048]{1,0:T(8,128)(2,1)}, u32[]{:S(2)}, u32[]{:S(2)}) collective-permute-start(bf16[192,2048]{1,0:T(8,128)(2,1)} %refs_0_.3), channel_id=1, source_target_pairs={{0,16},{1,17},{2,18},{3,19},{4,20},{5,21},{6,22},{7,23},{8,24},{9,... | collective-permute-start | bytes 2359304 | tf_op jit(solution)/shard_map/ppermute | solution.py:231
  80.0 34.9 %copy-start.1 = (bf16[192,1024]{1,0:T(8,128)(2,1)}, bf16[192,1024]{1,0:T(8,128)(2,1)S(1)}, u32[]{:S(2)}) copy-start(bf16[192,1024]{1,0:T(8,128)(2,1)S(1)} %collective-permute-done.10.refs_2_) | copy-start | bytes 1179652
  80.0 34.9 %collective-permute-start.8 = (bf16[192,1024]{1,0:T(8,128)(2,1)S(1)}, bf16[192,1024]{1,0:T(8,128)(2,1)S(1)}, u32[]{:S(2)}, u32[]{:S(2)}) collective-permute-start(bf16[192,1024]{1,0:T(8,128)(2,1)S(1)} %get-tuple-element.17), channel_id=1, source_target_pairs={{0,0},{1,1},{2,10},{3,11},{4,20},{5,21},{6,30},{7,31},{8,2},{9,3},... | collective-permute-start | bytes 1179656 | tf_op jit(solution)/shard_map/ppermute | solution.py:231
  88.4 26.6 %copy-start.2 = (bf16[192,1024]{1,0:T(8,128)(2,1)}, bf16[192,1024]{1,0:T(8,128)(2,1)S(1)}, u32[]{:S(2)}) copy-start(bf16[192,1024]{1,0:T(8,128)(2,1)S(1)} %collective-permute-done.11.refs_3_) | copy-start | bytes 1179652
  88.4 27.3 %collective-permute-start.9 = (bf16[192,1024]{1,0:T(8,128)(2,1)S(1)}, bf16[192,1024]{1,0:T(8,128)(2,1)}, u32[]{:S(2)}, u32[]{:S(2)}) collective-permute-start(bf16[192,1024]{1,0:T(8,128)(2,1)S(1)} %get-tuple-element.17), channel_id=1, source_target_pairs={{0,2},{1,3},{2,8},{3,9},{4,22},{5,23},{6,28},{7,29},{8,0},{9,1},{1... | collective-permute-start | bytes 1179656 | tf_op jit(solution)/shard_map/ppermute | solution.py:231
  114.9 0.7 copy-start.3
  120.7 42.5 %collective-permute-start.12 = (bf16[768,1024]{1,0:T(8,128)(2,1)}, bf16[768,1024]{1,0:T(8,128)(2,1)}, u32[]{:S(2)}, u32[]{:S(2)}) collective-permute-start(bf16[768,1024]{1,0:T(8,128)(2,1)} %residual.4.refs_0_), channel_id=1, source_target_pairs={{0,1},{1,0},{2,3},{3,2},{4,5},{5,4},{6,7},{7,6},{8,9},{9,8},{10,11... | collective-permute-start | bytes 4718600 | tf_op jit(solution)/shard_map/ppermute | solution.py:231
  121.7 11.6 %collective-permute-start.2 = (bf16[96,2048]{1,0:T(8,128)(2,1)S(1)}, bf16[96,2048]{1,0:T(8,128)(2,1)S(1)}, u32[]{:S(2)}, u32[]{:S(2)}) collective-permute-start(bf16[96,2048]{1,0:T(8,128)(2,1)S(1)} %slice.16), channel_id=1, source_target_pairs={{0,16},{1,17},{2,18},{3,19},{4,20},{5,21},{6,22},{7,23},{8,24},{9,... | collective-permute-start | bytes 1179656 | tf_op jit(solution)/shard_map/ppermute | solution.py:231
  124.4 11.4 %collective-permute-start.3 = (bf16[96,2048]{1,0:T(8,128)(2,1)S(1)}, bf16[96,2048]{1,0:T(8,128)(2,1)}, u32[]{:S(2)}, u32[]{:S(2)}) collective-permute-start(bf16[96,2048]{1,0:T(8,128)(2,1)S(1)} %slice.17), channel_id=1, source_target_pairs={{0,8},{1,9},{2,10},{3,11},{4,12},{5,13},{6,14},{7,15},{8,0},{9,1},... | collective-permute-start | bytes 1179656 | tf_op jit(solution)/shard_map/ppermute | solution.py:231
  133.3 0.7 copy-start

commit v2 on v1

--- a/solution.py
+++ b/solution.py
@@ -14,6 +14,8 @@
 CHUNKS = (1, 1)
 BF, F32 = jnp.bfloat16, jnp.float32
 VMEM_ALL = 67043328
+VMEM_MOST = 54525952
+VMEM_SOME = 33554432
 HIGHEST = lax.Precision.HIGHEST
 
 
@@ -146,7 +148,6 @@
     size, days = high.shape
     depth = days // order.shape[0]
     tile = min(tile, width)
-    whole = lambda shape: pl.BlockSpec(shape, lambda i, order: (0, 0))
     specs = [pl.BlockSpec((p.shape[0], tile), lambda i, order: (0, i)) for p in pieces]
     out_specs = [pl.BlockSpec((days, tile), lambda i, order: (0, i))]
     out_shape = [jax.ShapeDtypeStruct((days, width), BF)]
@@ -158,13 +159,13 @@
         grid_spec=pltpu.PrefetchScalarGridSpec(
             num_scalar_prefetch=1,
             grid=(width // tile,),
-            in_specs=specs + [whole((size, days))] * 2 + [whole((days, size))],
+            in_specs=specs + [pl.BlockSpec(memory_space=pltpu.VMEM)] * 3,
             out_specs=out_specs,
             scratch_shapes=[pltpu.VMEM((days, tile), BF)],
         ),
         out_shape=out_shape,
         cost_estimate=cost(6 * days * size * width, 4 * days * width),
-        compiler_params=pltpu.CompilerParams(vmem_limit_bytes=VMEM_ALL),
+        compiler_params=pltpu.CompilerParams(vmem_limit_bytes=VMEM_MOST),
         name="residual",
     )(order, *pieces, high, low, factors)
 
@@ -183,7 +184,7 @@
     width = parts[0].shape[1]
     tile = min(tile, width)
     count, tiles = len(parts), width // tile
-    specs = [pl.BlockSpec((depth, height), lambda k, j, where: (0, 0))]
+    specs = [pl.BlockSpec(memory_space=pltpu.VMEM)]
     for k in range(count):
         held_at = lambda s, j, where, k=k: (0, jnp.where(s == k, j, jnp.where(s < k, 0, tiles - 1)))
         specs.append(pl.BlockSpec((depth, tile), held_at))
@@ -204,7 +205,7 @@
         out_shape=jax.ShapeDtypeStruct((height, total), F32),
         input_output_aliases=aliases,
         cost_estimate=cost(2 * depth * height * width * count, 4 * height * width * count),
-        compiler_params=pltpu.CompilerParams(vmem_limit_bytes=VMEM_ALL),
+        compiler_params=pltpu.CompilerParams(vmem_limit_bytes=VMEM_SOME),
         name="covariance",
     )(jnp.stack([lax.div(s, tile) for s in starts]).astype(jnp.int32), *args)
 

time: 172 us -> 169 us (0.983)
  the two profiles are of different devices: /device:TPU:16 before, /device:TPU:0 now
where the time goes in v2:
time: 169 us; the launch traced here: 166 us
  waiting for transfers between devices  63.1 us (37%)
  Pallas kernels  49.8 us (29%)
  starting transfers between devices  38.8 us (23%)
  local copies, waits for them, and re-layouts  10.3 us (6%)
  other arithmetic  3.41 us (2%)
    ppermute x19, waiting for transfers between devices, move(): return lax.ppermute(x, AXES, pairs)  63.1 us
    ppermute x19, starting transfers between devices, move(): return lax.ppermute(x, AXES, pairs)  38.8 us
    pallas_call x3, Pallas kernels, covariance(): pl.pallas_call(functools.partial(covariance_kernel, 1.0 / days, count), g...  22.1 us
    pallas_call x3, Pallas kernels, residuals(): pl.pallas_call(functools.partial(residual_kernel, slots, depth, with_load...  15.1 us
    pallas_call x1, Pallas kernels, invert(): pl.pallas_call(functools.partial(invert_kernel, n), in_specs=[pl.BlockSpe...  12.6 us
    unnamed x24, local copies, waits for them, and re-layouts  6.75 us
  transfers between devices with their start and end apart: 19, of which 7 were waited for; matrix products, arithmetic and copies ran while one was open for 3% of the time, Pallas kernels for 26%

profile of v2, /device:TPU:0, one launch (start us, length us, event | category | flops | bytes accessed | tf_op | source)
XLA Modules:
  0.0 166.3 jit_solution(15333782762734489249)
XLA Ops:
  0.6 1.9 %fusion = (bf16[192,1024]{1,0:T(8,128)(2,1)S(1)}, bf16[192,1024]{1,0:T(8,128)(2,1)}) fusion(bf16[192,2048]{1,0:T(8,128)(2,1)} %refs_0_.3), kind=kLoop, calls=%fused_computation.7 | loop fusion | bytes 1572864 | tf_op jit(solution)/shard_map/slice | solution.py:267
  2.5 4.1 %collective-permute-start.13 = (bf16[192,1024]{1,0:T(8,128)(2,1)S(1)}, bf16[192,1024]{1,0:T(8,128)(2,1)S(1)}, u32[]{:S(2)}, u32[]{:S(2)}) collective-permute-start(bf16[192,1024]{1,0:T(8,128)(2,1)S(1)} %get-tuple-element.14), channel_id=1, source_target_pairs={{0,4},{1,5},{2,6},{3,7},{4,0},{5,1},{6,2},{7,3},{8,12},{9,13},{10,... | collective-permute-start | bytes 1179656 | tf_op jit(solution)/shard_map/ppermute | solution.py:232
  6.6 1.5 collective-permute-start.4
  8.1 1.5 collective-permute-start.5
  9.6 0.5 collective-permute-start.6
  10.1 0.7 pad_add_fusion.1.order
  10.8 0.6 pad_add_fusion.order
  11.3 22.1 %collective-permute-done.13 = bf16[192,1024]{1,0:T(8,128)(2,1)S(1)} collective-permute-done((bf16[192,1024]{1,0:T(8,128)(2,1)S(1)}, bf16[192,1024]{1,0:T(8,128)(2,1)S(1)}, u32[]{:S(2)}, u32[]{:S(2)}) %collective-permute-start.13) | collective-permute-done | bytes 393248 | tf_op jit(solution)/shard_map/ppermute | solution.py:232
  33.4 0.9 broadcast_select_fusion
  34.3 4.5 %collective-permute-start.14 = (bf16[192,1024]{1,0:T(8,128)(2,1)}, bf16[192,1024]{1,0:T(8,128)(2,1)}, u32[]{:S(2)}, u32[]{:S(2)}) collective-permute-start(bf16[192,1024]{1,0:T(8,128)(2,1)} %get-tuple-element.13), channel_id=1, source_target_pairs={{0,0},{1,1},{2,10},{3,11},{4,20},{5,21},{6,30},{7,31},{8,2},{9,3},... | collective-permute-start | bytes 1179656 | tf_op jit(solution)/shard_map/ppermute | solution.py:232
  38.8 0.0 collective-permute-done.4.refs_1_
  38.8 1.9 %collective-permute-start.15 = (bf16[192,1024]{1,0:T(8,128)(2,1)}, bf16[192,1024]{1,0:T(8,128)(2,1)}, u32[]{:S(2)}, u32[]{:S(2)}) collective-permute-start(bf16[192,1024]{1,0:T(8,128)(2,1)} %get-tuple-element.13), channel_id=1, source_target_pairs={{0,2},{1,3},{2,8},{3,9},{4,22},{5,23},{6,28},{7,29},{8,0},{9,1},{1... | collective-permute-start | bytes 1179656 | tf_op jit(solution)/shard_map/ppermute | solution.py:232
  40.7 0.0 collective-permute-done.5.refs_2_
  40.7 3.7 %collective-permute-start.16 = (bf16[192,1024]{1,0:T(8,128)(2,1)}, bf16[192,1024]{1,0:T(8,128)(2,1)}, u32[]{:S(2)}, u32[]{:S(2)}) collective-permute-start(bf16[192,1024]{1,0:T(8,128)(2,1)} %get-tuple-element.12), channel_id=1, source_target_pairs={{0,16},{1,17},{2,26},{3,27},{4,4},{5,5},{6,14},{7,15},{8,18},{9,19... | collective-permute-start | bytes 1179656 | tf_op jit(solution)/shard_map/ppermute | solution.py:232
  44.5 0.0 collective-permute-done.6.refs_3_
  44.5 4.8 %collective-permute-start.17 = (bf16[192,1024]{1,0:T(8,128)(2,1)}, bf16[192,1024]{1,0:T(8,128)(2,1)}, u32[]{:S(2)}, u32[]{:S(2)}) collective-permute-start(bf16[192,1024]{1,0:T(8,128)(2,1)} %get-tuple-element.12), channel_id=1, source_target_pairs={{0,18},{1,19},{2,24},{3,25},{4,6},{5,7},{6,12},{7,13},{8,16},{9,17... | collective-permute-start | bytes 1179656 | tf_op jit(solution)/shard_map/ppermute | solution.py:232
  49.3 12.6 %gram.1 = (bf16[768,256]{1,0:T(8,128)(2,1)}, bf16[256,768]{1,0:T(8,128)(2,1)}, bf16[256,768]{1,0:T(8,128)(2,1)}) custom-call(s32[4]{0:T(128)} %pad_add_fusion.order, bf16[192,256]{1,0:T(8,128)(2,1)} %refs_0_.2, bf16[192,256]{1,0:T(8,128)(2,1)} %collective-permute-done.4.refs_1_, bf16[192,256]{1,0:T(8,128)(2,1)} %collective-permute-done.5.refs_2_, ...), custom_call_target="tpu_custom_call" | custom-call | flops 20000000000 | bytes 1572864 | tf_op jit(solution)/shard_map/gram/pallas_call | solution.py:120
  61.9 0.7 collective-permute-done.17.refs_3_
  62.6 0.7 copy-done.4
  63.3 1.0 copy-done.6
  64.3 4.8 %residual.5.refs_0_ = bf16[768,1024]{1,0:T(8,128)(2,1)} custom-call(s32[4]{0:T(128)S(1)} %copy-done.4, bf16[192,1024]{1,0:T(8,128)(2,1)} %collective-permute-done.14.refs_0_, bf16[192,1024]{1,0:T(8,128)(2,1)} %collective-permute-done.15.refs_1_, bf16[192,1024]{1,0:T(8,128)(2,1)} %collective-permute-done.16.refs_2_, ...), custom_call_target="tpu_custom_call" | custom-call | flops 1207959552 | bytes 3145728 | tf_op jit(solution)/shard_map/residual/pallas_call | solution.py:157
  69.1 1.2 broadcast_select_fusion.2
  70.3 3.3 %collective-permute-start.10 = (bf16[192,1024]{1,0:T(8,128)(2,1)S(1)}, bf16[192,1024]{1,0:T(8,128)(2,1)S(1)}, u32[]{:S(2)}, u32[]{:S(2)}) collective-permute-start(bf16[192,1024]{1,0:T(8,128)(2,1)S(1)} %get-tuple-element.16), channel_id=1, source_target_pairs={{0,16},{1,17},{2,26},{3,27},{4,4},{5,5},{6,14},{7,15},{8,18},{9,19... | collective-permute-start | bytes 1179656 | tf_op jit(solution)/shard_map/ppermute | solution.py:232
  73.6 5.7 %collective-permute-start.11 = (bf16[192,1024]{1,0:T(8,128)(2,1)S(1)}, bf16[192,1024]{1,0:T(8,128)(2,1)S(1)}, u32[]{:S(2)}, u32[]{:S(2)}) collective-permute-start(bf16[192,1024]{1,0:T(8,128)(2,1)S(1)} %get-tuple-element.16), channel_id=1, source_target_pairs={{0,18},{1,19},{2,24},{3,25},{4,6},{5,7},{6,12},{7,13},{8,16},{9,17... | collective-permute-start | bytes 1179656 | tf_op jit(solution)/shard_map/ppermute | solution.py:232
  79.3 0.6 collective-permute-start
  80.0 1.0 collective-permute-start.1
  81.0 11.6 %collective-permute-done.10.refs_2_ = bf16[192,1024]{1,0:T(8,128)(2,1)S(1)} collective-permute-done((bf16[192,1024]{1,0:T(8,128)(2,1)S(1)}, bf16[192,1024]{1,0:T(8,128)(2,1)S(1)}, u32[]{:S(2)}, u32[]{:S(2)}) %collective-permute-start.10) | collective-permute-done | bytes 393248 | tf_op jit(solution)/shard_map/ppermute | solution.py:232
  92.6 0.8 collective-permute-start.8
  93.4 1.8 %collective-permute-done.11.refs_3_ = bf16[192,1024]{1,0:T(8,128)(2,1)S(1)} collective-permute-done((bf16[192,1024]{1,0:T(8,128)(2,1)S(1)}, bf16[192,1024]{1,0:T(8,128)(2,1)S(1)}, u32[]{:S(2)}, u32[]{:S(2)}) %collective-permute-start.11) | collective-permute-done | bytes 393248 | tf_op jit(solution)/shard_map/ppermute | solution.py:232
  95.2 4.4 %collective-permute-start.9 = (bf16[192,1024]{1,0:T(8,128)(2,1)S(1)}, bf16[192,1024]{1,0:T(8,128)(2,1)S(1)}, u32[]{:S(2)}, u32[]{:S(2)}) collective-permute-start(bf16[192,1024]{1,0:T(8,128)(2,1)S(1)} %get-tuple-element.17), channel_id=1, source_target_pairs={{0,2},{1,3},{2,8},{3,9},{4,22},{5,23},{6,28},{7,29},{8,0},{9,1},{1... | collective-permute-start | bytes 1179656 | tf_op jit(solution)/shard_map/ppermute | solution.py:232
  99.6 15.4 %collective-permute-done.9.refs_1_ = bf16[192,1024]{1,0:T(8,128)(2,1)S(1)} collective-permute-done((bf16[192,1024]{1,0:T(8,128)(2,1)S(1)}, bf16[192,1024]{1,0:T(8,128)(2,1)S(1)}, u32[]{:S(2)}, u32[]{:S(2)}) %collective-permute-start.9) | collective-permute-done | bytes 393248 | tf_op jit(solution)/shard_map/ppermute | solution.py:232
  115.0 4.3 %residual.4.refs_0_ = bf16[768,1024]{1,0:T(8,128)(2,1)} custom-call(s32[4]{0:T(128)S(1)} %copy-done.4, bf16[192,1024]{1,0:T(8,128)(2,1)S(1)} %collective-permute-done.8.refs_0_, bf16[192,1024]{1,0:T(8,128)(2,1)S(1)} %collective-permute-done.9.refs_1_, bf16[192,1024]{1,0:T(8,128)(2,1)S(1)} %collective-permute-done.10.refs_2_, ...), custom_call_target="tpu_custom_call" | custom-call | flops 1207959552 | bytes 3145728 | tf_op jit(solution)/shard_map/residual/pallas_call | solution.py:157
  119.3 0.8 slice.16
  120.1 0.5 collective-permute-start.2
  120.7 0.8 slice.17
  121.5 0.2 copy-done.11
  121.7 0.1 pad_add_fusion.2.where
  121.8 10.1 %collective-permute-done.2.refs_3_ = bf16[96,2048]{1,0:T(8,128)(2,1)S(1)} collective-permute-done((bf16[96,2048]{1,0:T(8,128)(2,1)}, bf16[96,2048]{1,0:T(8,128)(2,1)S(1)}, u32[]{:S(2)}, u32[]{:S(2)}) %collective-permute-start.2) | collective-permute-done | bytes 393248 | tf_op jit(solution)/shard_map/ppermute | solution.py:232
  131.9 1.4 collective-permute-done.3.refs_4_
  133.3 1.0 copy-done.5
  134.3 1.0 copy-done.7
  135.2 1.0 copy-done.8
  136.2 6.0 %residual.3 = (bf16[768,2048]{1,0:T(8,128)(2,1)}, f32[256,2048]{1,0:T(8,128)}) custom-call(s32[4]{0:T(128)S(1)} %copy-done.3, bf16[192,2048]{1,0:T(8,128)(2,1)} %refs_0_.3, bf16[192,2048]{1,0:T(8,128)(2,1)} %copy-done.10, bf16[192,2048]{1,0:T(8,128)(2,1)} %copy-done.11, bf16[96,2048]{1,0:T(8,128)(2,1)S(1)} %collective-permute-done.2.refs_3_, ...), custom_call_target="tpu_custom_call" | custom-call | flops 2415919104 | bytes 6291456 | tf_op jit(solution)/shard_map/residual/pallas_call | solution.py:157
  142.3 0.0 copy-start
  142.3 1.9 %copy-done = bf16[768,2048]{1,0:T(8,128)(2,1)S(1)} copy-done((bf16[768,2048]{1,0:T(8,128)(2,1)S(1)}, bf16[768,2048]{1,0:T(8,128)(2,1)}, u32[]{:S(2)}) %copy-start) | copy-done | bytes 3145752
  144.2 10.4 %covariance.3.refs_1_ = f32[2048,4096]{1,0:T(8,128)} custom-call(s32[2]{0:T(128)S(1)} %pad_add_fusion.2.where, bf16[768,2048]{1,0:T(8,128)(2,1)S(1)} %copy-done, bf16[768,1024]{1,0:T(8,128)(2,1)S(1)} %copy-done.1, bf16[768,1024]{1,0:T(8,128)(2,1)S(1)} %collective-permute-done.18.refs_1_), custom_call_target="tpu_custom_call" | custom-call | flops 6442450944 | bytes 16777216 | tf_op jit(solution)/shard_map/covariance/pallas_call | solution.py:197
  154.6 5.8 %covariance.4.refs_1_ = f32[2048,4096]{1,0:T(8,128)} custom-call(s32[1]{0:T(128)} %bitcast.9.where, bf16[768,2048]{1,0:T(8,128)(2,1)S(1)} %copy-done, bf16[768,1024]{1,0:T(8,128)(2,1)S(1)} %copy-done.2, f32[2048,4096]{1,0:T(8,128)} %covariance.3.refs_1_), custom_call_target="tpu_custom_call", output_to_operand_aliasing={{}: (3, {})} | custom-call | flops 3221225472 | bytes 8388608 | tf_op jit(solution)/shard_map/covariance/pallas_call | solution.py:197
  160.4 5.8 %covariance.5 = f32[2048,4096]{1,0:T(8,128)} custom-call(s32[1]{0:T(128)} %bitcast.4.where, bf16[768,2048]{1,0:T(8,128)(2,1)S(1)} %copy-done, bf16[768,1024]{1,0:T(8,128)(2,1)S(1)} %collective-permute-done.12.refs_0_, f32[2048,4096]{1,0:T(8,128)} %covariance.4.refs_1_), custom_call_target="tpu_custom_call", output_to_operand_aliasing={{}: (3, {})} | custom-call | flops 3221225472 | bytes 8388608 | tf_op jit(solution)/shard_map/covariance/pallas_call | solution.py:197
  (29 shorter events, 0.1 us)
Async XLA Ops:
  2.5 30.9 %collective-permute-start.13 = (bf16[192,1024]{1,0:T(8,128)(2,1)S(1)}, bf16[192,1024]{1,0:T(8,128)(2,1)S(1)}, u32[]{:S(2)}, u32[]{:S(2)}) collective-permute-start(bf16[192,1024]{1,0:T(8,128)(2,1)S(1)} %get-tuple-element.14), channel_id=1, source_target_pairs={{0,4},{1,5},{2,6},{3,7},{4,0},{5,1},{6,2},{7,3},{8,12},{9,13},{10,... | collective-permute-start | bytes 1179656 | tf_op jit(solution)/shard_map/ppermute | solution.py:232
  6.6 32.2 %collective-permute-start.4 = (bf16[192,256]{1,0:T(8,128)(2,1)}, bf16[192,256]{1,0:T(8,128)(2,1)}, u32[]{:S(2)}, u32[]{:S(2)}) collective-permute-start(bf16[192,256]{1,0:T(8,128)(2,1)} %refs_0_.2), channel_id=1, source_target_pairs={{0,8},{1,9},{2,10},{3,11},{4,12},{5,13},{6,14},{7,15},{8,0},{9,1},... | collective-permute-start | bytes 294920 | tf_op jit(solution)/shard_map/ppermute | solution.py:232
  8.1 32.6 %collective-permute-start.5 = (bf16[192,256]{1,0:T(8,128)(2,1)}, bf16[192,256]{1,0:T(8,128)(2,1)}, u32[]{:S(2)}, u32[]{:S(2)}) collective-permute-start(bf16[192,256]{1,0:T(8,128)(2,1)} %refs_0_.2), channel_id=1, source_target_pairs={{0,16},{1,17},{2,18},{3,19},{4,20},{5,21},{6,22},{7,23},{8,24},{9,... | collective-permute-start | bytes 294920 | tf_op jit(solution)/shard_map/ppermute | solution.py:232
  9.6 34.9 %collective-permute-start.6 = (bf16[192,256]{1,0:T(8,128)(2,1)}, bf16[192,256]{1,0:T(8,128)(2,1)}, u32[]{:S(2)}, u32[]{:S(2)}) collective-permute-start(bf16[192,256]{1,0:T(8,128)(2,1)} %refs_0_.2), channel_id=1, source_target_pairs={{0,24},{1,25},{2,26},{3,27},{4,28},{5,29},{6,30},{7,31},{8,16},{9,... | collective-permute-start | bytes 294920 | tf_op jit(solution)/shard_map/ppermute | solution.py:232
  10.1 59.0 %collective-permute-start.7 = (bf16[192,1024]{1,0:T(8,128)(2,1)}, bf16[192,1024]{1,0:T(8,128)(2,1)}, u32[]{:S(2)}, u32[]{:S(2)}) collective-permute-start(bf16[192,1024]{1,0:T(8,128)(2,1)} %get-tuple-element.15), channel_id=1, source_target_pairs={{0,4},{1,5},{2,6},{3,7},{4,0},{5,1},{6,2},{7,3},{8,12},{9,13},{10,... | collective-permute-start | bytes 1179656 | tf_op jit(solution)/shard_map/ppermute | solution.py:232
  34.3 27.5 %collective-permute-start.14 = (bf16[192,1024]{1,0:T(8,128)(2,1)}, bf16[192,1024]{1,0:T(8,128)(2,1)}, u32[]{:S(2)}, u32[]{:S(2)}) collective-permute-start(bf16[192,1024]{1,0:T(8,128)(2,1)} %get-tuple-element.13), channel_id=1, source_target_pairs={{0,0},{1,1},{2,10},{3,11},{4,20},{5,21},{6,30},{7,31},{8,2},{9,3},... | collective-permute-start | bytes 1179656 | tf_op jit(solution)/shard_map/ppermute | solution.py:232
  38.8 23.1 %collective-permute-start.15 = (bf16[192,1024]{1,0:T(8,128)(2,1)}, bf16[192,1024]{1,0:T(8,128)(2,1)}, u32[]{:S(2)}, u32[]{:S(2)}) collective-permute-start(bf16[192,1024]{1,0:T(8,128)(2,1)} %get-tuple-element.13), channel_id=1, source_target_pairs={{0,2},{1,3},{2,8},{3,9},{4,22},{5,23},{6,28},{7,29},{8,0},{9,1},{1... | collective-permute-start | bytes 1179656 | tf_op jit(solution)/shard_map/ppermute | solution.py:232
  40.7 21.2 %collective-permute-start.16 = (bf16[192,1024]{1,0:T(8,128)(2,1)}, bf16[192,1024]{1,0:T(8,128)(2,1)}, u32[]{:S(2)}, u32[]{:S(2)}) collective-permute-start(bf16[192,1024]{1,0:T(8,128)(2,1)} %get-tuple-element.12), channel_id=1, source_target_pairs={{0,16},{1,17},{2,26},{3,27},{4,4},{5,5},{6,14},{7,15},{8,18},{9,19... | collective-permute-start | bytes 1179656 | tf_op jit(solution)/shard_map/ppermute | solution.py:232
  44.5 18.1 %collective-permute-start.17 = (bf16[192,1024]{1,0:T(8,128)(2,1)}, bf16[192,1024]{1,0:T(8,128)(2,1)}, u32[]{:S(2)}, u32[]{:S(2)}) collective-permute-start(bf16[192,1024]{1,0:T(8,128)(2,1)} %get-tuple-element.12), channel_id=1, source_target_pairs={{0,18},{1,19},{2,24},{3,25},{4,6},{5,7},{6,12},{7,13},{8,16},{9,17... | collective-permute-start | bytes 1179656 | tf_op jit(solution)/shard_map/ppermute | solution.py:232
  62.6 0.7 copy-start.4
  63.3 1.0 copy-start.6
  64.3 15.0 %copy-start.9 = (bf16[192,2048]{1,0:T(8,128)(2,1)S(1)}, bf16[192,2048]{1,0:T(8,128)(2,1)}, u32[]{:S(2)}) copy-start(bf16[192,2048]{1,0:T(8,128)(2,1)} %refs_0_.3) | copy-start | bytes 2359300
  69.1 73.2 %collective-permute-start.18 = (bf16[768,1024]{1,0:T(8,128)(2,1)}, bf16[768,1024]{1,0:T(8,128)(2,1)S(1)}, u32[]{:S(2)}, u32[]{:S(2)}) collective-permute-start(bf16[768,1024]{1,0:T(8,128)(2,1)} %residual.5.refs_0_), channel_id=1, source_target_pairs={{0,1},{1,0},{2,3},{3,2},{4,5},{5,4},{6,7},{7,6},{8,9},{9,8},{10,11... | collective-permute-start | bytes 4718600 | tf_op jit(solution)/shard_map/ppermute | solution.py:232
  70.3 22.3 %collective-permute-start.10 = (bf16[192,1024]{1,0:T(8,128)(2,1)S(1)}, bf16[192,1024]{1,0:T(8,128)(2,1)S(1)}, u32[]{:S(2)}, u32[]{:S(2)}) collective-permute-start(bf16[192,1024]{1,0:T(8,128)(2,1)S(1)} %get-tuple-element.16), channel_id=1, source_target_pairs={{0,16},{1,17},{2,26},{3,27},{4,4},{5,5},{6,14},{7,15},{8,18},{9,19... | collective-permute-start | bytes 1179656 | tf_op jit(solution)/shard_map/ppermute | solution.py:232
  73.6 21.5 %collective-permute-start.11 = (bf16[192,1024]{1,0:T(8,128)(2,1)S(1)}, bf16[192,1024]{1,0:T(8,128)(2,1)S(1)}, u32[]{:S(2)}, u32[]{:S(2)}) collective-permute-start(bf16[192,1024]{1,0:T(8,128)(2,1)S(1)} %get-tuple-element.16), channel_id=1, source_target_pairs={{0,18},{1,19},{2,24},{3,25},{4,6},{5,7},{6,12},{7,13},{8,16},{9,17... | collective-permute-start | bytes 1179656 | tf_op jit(solution)/shard_map/ppermute | solution.py:232
  79.3 40.0 %collective-permute-start = (bf16[192,2048]{1,0:T(8,128)(2,1)S(1)}, bf16[192,2048]{1,0:T(8,128)(2,1)S(1)}, u32[]{:S(2)}, u32[]{:S(2)}) collective-permute-start(bf16[192,2048]{1,0:T(8,128)(2,1)S(1)} %copy-done.9), channel_id=1, source_target_pairs={{0,8},{1,9},{2,10},{3,11},{4,12},{5,13},{6,14},{7,15},{8,0},{9,1},... | collective-permute-start | bytes 2359304 | tf_op jit(solution)/shard_map/ppermute | solution.py:232
  80.0 40.7 %collective-permute-start.1 = (bf16[192,2048]{1,0:T(8,128)(2,1)S(1)}, bf16[192,2048]{1,0:T(8,128)(2,1)S(1)}, u32[]{:S(2)}, u32[]{:S(2)}) collective-permute-start(bf16[192,2048]{1,0:T(8,128)(2,1)S(1)} %copy-done.9), channel_id=1, source_target_pairs={{0,16},{1,17},{2,18},{3,19},{4,20},{5,21},{6,22},{7,23},{8,24},{9,... | collective-permute-start | bytes 2359304 | tf_op jit(solution)/shard_map/ppermute | solution.py:232
  92.6 40.6 %copy-start.3 = (s32[4]{0:T(128)S(1)}, s32[4]{0:T(128)}, u32[]{:S(2)}) copy-start(s32[4]{0:T(128)} %pad_add_fusion.order) | copy-start | bytes 52
  92.6 7.0 %collective-permute-start.8 = (bf16[192,1024]{1,0:T(8,128)(2,1)S(1)}, bf16[192,1024]{1,0:T(8,128)(2,1)S(1)}, u32[]{:S(2)}, u32[]{:S(2)}) collective-permute-start(bf16[192,1024]{1,0:T(8,128)(2,1)S(1)} %get-tuple-element.17), channel_id=1, source_target_pairs={{0,0},{1,1},{2,10},{3,11},{4,20},{5,21},{6,30},{7,31},{8,2},{9,3},... | collective-permute-start | bytes 1179656 | tf_op jit(solution)/shard_map/ppermute | solution.py:232
  95.2 19.8 %collective-permute-start.9 = (bf16[192,1024]{1,0:T(8,128)(2,1)S(1)}, bf16[192,1024]{1,0:T(8,128)(2,1)S(1)}, u32[]{:S(2)}, u32[]{:S(2)}) collective-permute-start(bf16[192,1024]{1,0:T(8,128)(2,1)S(1)} %get-tuple-element.17), channel_id=1, source_target_pairs={{0,2},{1,3},{2,8},{3,9},{4,22},{5,23},{6,28},{7,29},{8,0},{9,1},{1... | collective-permute-start | bytes 1179656 | tf_op jit(solution)/shard_map/ppermute | solution.py:232
  119.3 41.1 %collective-permute-start.12 = (bf16[768,1024]{1,0:T(8,128)(2,1)}, bf16[768,1024]{1,0:T(8,128)(2,1)S(1)}, u32[]{:S(2)}, u32[]{:S(2)}) collective-permute-start(bf16[768,1024]{1,0:T(8,128)(2,1)} %residual.4.refs_0_), channel_id=1, source_target_pairs={{0,1},{1,0},{2,3},{3,2},{4,5},{5,4},{6,7},{7,6},{8,9},{9,8},{10,11... | collective-permute-start | bytes 4718600 | tf_op jit(solution)/shard_map/ppermute | solution.py:232
  119.3 1.4 copy-start.10
  120.1 11.7 %collective-permute-start.2 = (bf16[96,2048]{1,0:T(8,128)(2,1)}, bf16[96,2048]{1,0:T(8,128)(2,1)S(1)}, u32[]{:S(2)}, u32[]{:S(2)}) collective-permute-start(bf16[96,2048]{1,0:T(8,128)(2,1)} %slice.16), channel_id=1, source_target_pairs={{0,16},{1,17},{2,18},{3,19},{4,20},{5,21},{6,22},{7,23},{8,24},{9,... | collective-permute-start | bytes 1179656 | tf_op jit(solution)/shard_map/ppermute | solution.py:232
  120.6 1.0 copy-start.11
  121.7 11.6 %collective-permute-start.3 = (bf16[96,2048]{1,0:T(8,128)(2,1)}, bf16[96,2048]{1,0:T(8,128)(2,1)}, u32[]{:S(2)}, u32[]{:S(2)}) collective-permute-start(bf16[96,2048]{1,0:T(8,128)(2,1)} %slice.17), channel_id=1, source_target_pairs={{0,8},{1,9},{2,10},{3,11},{4,12},{5,13},{6,14},{7,15},{8,0},{9,1},... | collective-permute-start | bytes 1179656 | tf_op jit(solution)/shard_map/ppermute | solution.py:232
  121.8 20.5 %copy-start.1 = (bf16[768,1024]{1,0:T(8,128)(2,1)S(1)}, bf16[768,1024]{1,0:T(8,128)(2,1)}, u32[]{:S(2)}) copy-start(bf16[768,1024]{1,0:T(8,128)(2,1)} %residual.5.refs_0_) | copy-start | bytes 4718596
  133.3 1.0 copy-start.5
  134.3 1.0 copy-start.7
  135.2 1.0 copy-start.8
  142.3 1.9 %copy-start = (bf16[768,2048]{1,0:T(8,128)(2,1)S(1)}, bf16[768,2048]{1,0:T(8,128)(2,1)}, u32[]{:S(2)}) copy-start(bf16[768,2048]{1,0:T(8,128)(2,1)} %get-tuple-element.11.rows) | copy-start | bytes 9437188
  144.2 10.4 %copy-start.2 = (bf16[768,1024]{1,0:T(8,128)(2,1)S(1)}, bf16[768,1024]{1,0:T(8,128)(2,1)}, u32[]{:S(2)}) copy-start(bf16[768,1024]{1,0:T(8,128)(2,1)} %residual.4.refs_0_) | copy-start | bytes 4718596
